TPU v7x, 32 devices: a whole 2x2x4 slice. The times are simulated.
32 devices in a mesh: pipe: 8 (over z, x), fsdp: 4 (over y, core).
Axes of the slice: x: 2, y: 2, z: 4, core: 2. Of those that a mesh axis runs over, the one named last changes fastest.
Arguments:
- frames_in: bfloat16 [64, 384, 768], P(('pipe', 'fsdp')), may hold values from -6 to 6
- attn_in: bfloat16 [2, 768, 2304], P(None, 'fsdp'), may hold values from -0.21875 to 0.21875
- q_bias: bfloat16 [2, 768], P(None, 'fsdp'), may hold values from -1.796875 to 1.796875
- attn_out: bfloat16 [2, 768, 768], P(None, 'fsdp'), may hold values from -2.5 to 2.5
- out_bias: bfloat16 [2, 768], P(None, 'fsdp'), may hold values from -1.796875 to 1.796875
- norm1_gain: bfloat16 [2, 768], P(None, 'fsdp'), may hold values from 0.5 to 1.5
- norm1_bias: bfloat16 [2, 768], P(None, 'fsdp'), may hold values from -1.796875 to 1.796875
- ffn_up: bfloat16 [2, 768, 3072], P(None, 'fsdp'), may hold values from -0.21875 to 0.21875
- up_bias: bfloat16 [2, 3072], P(None, 'fsdp'), may hold values from -1.796875 to 1.796875
- ffn_down: bfloat16 [2, 3072, 768], P(None, 'fsdp'), may hold values from -0.21875 to 0.21875
- down_bias: bfloat16 [2, 768], P(None, 'fsdp'), may hold values from -1.796875 to 1.796875
- norm2_gain: bfloat16 [2, 768], P(None, 'fsdp'), may hold values from 0.5 to 1.5
- norm2_bias: bfloat16 [2, 768], P(None, 'fsdp'), may hold values from -1.796875 to 1.796875
- subnet: int32 [4, 4], replicated, may hold values from 0 to 2, as said below
- out_cotangent: bfloat16 [64, 384, 768], P(('pipe', 'fsdp')), may hold values from -6 to 6
Outputs:
- layer_out: bfloat16 [64, 384, 768], P(('pipe', 'fsdp'))
- input_grad: bfloat16 [64, 384, 768], P(('pipe', 'fsdp'))
- grad_attn_in: float32 [2, 768, 2304], P(None, 'fsdp')
- grad_q_bias: float32 [2, 768], P(None, 'fsdp')
- grad_attn_out: float32 [2, 768, 768], P(None, 'fsdp')
- grad_out_bias: float32 [2, 768], P(None, 'fsdp')
- grad_norm1_gain: float32 [2, 768], P(None, 'fsdp')
- grad_norm1_bias: float32 [2, 768], P(None, 'fsdp')
- grad_ffn_up: float32 [2, 768, 3072], P(None, 'fsdp')
- grad_up_bias: float32 [2, 3072], P(None, 'fsdp')
- grad_ffn_down: float32 [2, 3072, 768], P(None, 'fsdp')
- grad_down_bias: float32 [2, 768], P(None, 'fsdp')
- grad_norm2_gain: float32 [2, 768], P(None, 'fsdp')
- grad_norm2_bias: float32 [2, 768], P(None, 'fsdp')
Inputs may be any that keep to these rules, and one draw needn't show every extreme that they name: `subnet`: rows 0, 1 and 2 hold indices of width, head count and feed-forward ratio; row 3 holds the skip flag. Exactly one micro-batch has skip flag 1, and some micro-batch with skip flag 0 has index 2 in rows 0, 1 and 2.
All inputs are finite; a program needn't handle non-finite values.
Results may differ from a plain program's by a relative error of at most 0.02.
Values may be sent and summed in bfloat16 or wider, within the bound.
A program may use at most 256 MiB of HBM per device.

v0:
```python
import functools

import jax
import jax.numpy as jnp
from jax import lax
from jax.experimental import pallas as pl
from jax.experimental.pallas import tpu as pltpu
from jax.sharding import PartitionSpec as P

HEADS = 12
HEAD_DIM = 64
EPSILON = 1e-05
LANES = 128
UNIT_CHUNK = 512
BF = jnp.bfloat16
F32 = jnp.float32

ROW_QB, ROW_OB, ROW_G1, ROW_B1, ROW_DB, ROW_G2, ROW_B2, ROW_UB = 0, 1, 2, 3, 4, 5, 6, 7

def dot_nn(a, b):
    return lax.dot_general(a, b, (((1,), (0,)), ((), ())), preferred_element_type=F32)


def dot_nt(a, b):
    return lax.dot_general(a, b, (((1,), (1,)), ((), ())), preferred_element_type=F32)


def dot_tn(a, b):
    return lax.dot_general(a, b, (((0,), (0,)), ((), ())), preferred_element_type=F32)


def lane_mask(width, count):
    return (lax.broadcasted_iota(jnp.int32, (1, width), 1) < count).astype(F32)


def normed(rows, cm, inv_w):
    mean = jnp.sum(rows * cm, axis=-1, keepdims=True) * inv_w
    centered = (rows - mean) * cm
    var = jnp.sum(centered * centered, axis=-1, keepdims=True) * inv_w
    rstd = lax.rsqrt(var + EPSILON)
    return centered * rstd, rstd


def norm_back(dy, xhat, rstd, gain, cm, inv_w):
    dym = dy * cm
    dg = jnp.sum(dym * xhat, axis=0, keepdims=True)
    ds = jnp.sum(dym, axis=0, keepdims=True)
    dx = dym * gain
    m1 = jnp.sum(dx, axis=-1, keepdims=True) * inv_w
    m2 = jnp.sum(dx * xhat, axis=-1, keepdims=True) * inv_w
    return cm * (rstd * (dx - m1 - xhat * m2)), dg, ds


class Attn:
    def __init__(self, layer, refs, w, sems):
        w_in, w_out = refs
        d = w.shape[1]
        self.copies = [
            pltpu.make_async_copy(w_in.at[layer, :, pl.ds(b * d, d)], w.at[b], sems.at[b]) for b in range(3)
        ] + [pltpu.make_async_copy(w_out.at[layer], w.at[3], sems.at[3])]

    def start(self, order):
        for b in order:
            self.copies[b].start()

    def wait(self, b):
        self.copies[b].wait()


class Ffn:
    def __init__(self, layer, refs, w_up, w_down, sems):
        up, down = refs
        d = w_up.shape[0]
        self.blocks = w_up.shape[1] // d
        self.first = [b * d // UNIT_CHUNK for b in range(self.blocks)]
        self.copies = [(
            pltpu.make_async_copy(up.at[layer, :, pl.ds(b * d, d)], w_up.at[:, pl.ds(b * d, d)], sems.at[b, 0]),
            pltpu.make_async_copy(down.at[layer, pl.ds(b * d, d)], w_down.at[pl.ds(b * d, d)], sems.at[b, 1]),
        ) for b in range(self.blocks)]

    def start(self):
        for pair in self.copies:
            for copy in pair:
                copy.start()

    def wait(self, b):
        for copy in self.copies[b]:
            copy.wait()

    def before(self, c):
        for b in range(self.blocks):
            @pl.when(c == self.first[b])
            def _(b=b):
                self.wait(b)

    def drain(self, counts):
        most = jnp.maximum(counts[0], counts[1])
        for b in range(self.blocks):
            @pl.when(most <= self.first[b])
            def _(b=b):
                self.wait(b)


class Table:
    def __init__(self, subnet, items, width):
        segment = lax.axis_index("pipe") // (lax.axis_size("pipe") // 2)
        codes = [[subnet[k, segment * items + i] for k in range(4)] for i in range(items)]
        widths = [width * (4 + k) // 6 for k in range(3)]
        self.w = [width * (4 + c[0]) // 6 for c in codes]
        self.inv = [
            jnp.where(c[0] == 0, 1.0 / widths[0], jnp.where(c[0] == 1, 1.0 / widths[1], 1.0 / widths[2])) for c in codes]
        self.a = [HEAD_DIM * (HEADS * (4 + c[1]) // 6) for c in codes]
        self.u = [w * (6 + c[2]) // 2 for w, c in zip(self.w, codes)]
        self.skip = [c[3] for c in codes]
        self.pairs = [(a + LANES - 1) // LANES for a in self.a]
        self.chunks = [(u + UNIT_CHUNK - 1) // UNIT_CHUNK for u in self.u]


def fetch(src, dst, sem):
    copy = pltpu.make_async_copy(src, dst, sem)
    copy.start()
    return copy


def pick(i, values):
    return values[i] if isinstance(i, int) else jnp.where(i == 0, values[0], values[1])


def rows_of(i, frames):
    if isinstance(i, int):
        return pl.ds(i * frames, frames)
    return pl.ds(pl.multiple_of(i * frames, frames), frames)


def over_both(counts, body):
    n0, n1 = counts
    low, high = jnp.minimum(n0, n1), jnp.maximum(n0, n1)
    longer = (n1 > n0).astype(jnp.int32)

    def both(c, _):
        body((0, 1), c)
        return 0

    def one(c, _):
        body((longer,), c)
        return 0

    lax.fori_loop(0, low, both, 0)
    lax.fori_loop(low, high, one, 0)


def mask_rows(x, items, frames, tab):
    for i in range(items):
        rr = rows_of(i, frames)
        x[rr, :] = jnp.where(lane_mask(x.shape[1], tab.w[i]) > 0, x[rr, :], jnp.zeros((), x.dtype))


def half_mask(h):
    low = lax.broadcasted_iota(jnp.int32, (1, LANES), 1) < HEAD_DIM
    return low if h == 0 else jnp.logical_not(low)


def only(h, x):
    return jnp.where(half_mask(h), x, jnp.zeros_like(x))


def attn_front(layer, items, frames, tab, vec, buf, weights, sems, outs, hooks):
    w, x, qkv, pt, ob, r1 = buf
    wsem, sem, ptsem = sems
    qkv_o, pt_o, ob_o, r1_o = outs
    width = x.shape[1]
    npair = width // LANES
    p = Attn(layer, weights, w, wsem)
    p.start((0, 1, 2, 3))
    cms = [lane_mask(width, n) for n in tab.w]
    hms = [lane_mask(width, n) for n in tab.a]
    done = []
    for j in range(3):
        p.wait(j)
        accs = [dot_nn(x[rows_of(i, frames), :], w[j]) for i in range(items)]
        for i, acc in enumerate(accs):
            if j == 0:
                acc = acc + vec[layer, ROW_QB:ROW_QB + 1, :]
            qkv[j, rows_of(i, frames), :] = (acc * hms[i]).astype(BF)
        done.append(fetch(qkv.at[j], qkv_o.at[j], sem.at[j]))

    def store(c):
        return pltpu.make_async_copy(pt.at[:, pl.ds(2 * c, 2)], pt_o.at[:, pl.ds(2 * c, 2)], ptsem.at[c])

    def pair(c, _):
        for at, hook in hooks.items():
            @pl.when(c == at)
            def _(hook=hook):
                hook()

        lanes = pl.ds(pl.multiple_of(c * LANES, LANES), LANES)
        vts, ss = [], []
        for i in range(items):
            rr = rows_of(i, frames)
            q = qkv[0, rr, lanes] * jnp.asarray(HEAD_DIM ** -0.5, BF)
            k = qkv[1, rr, lanes]
            vts.append(qkv[2, rr, lanes].T)
            ss += [dot_nt(only(h, k), q) for h in (0, 1)]
        es = [jnp.exp(s - jnp.max(s, axis=0, keepdims=True)) for s in ss]
        pbs = [(e * (1.0 / jnp.sum(e, axis=0, keepdims=True))).astype(BF) for e in es]
        for i in range(items):
            mixed = []
            for h in (0, 1):
                pt[i, 2 * c + h] = pbs[2 * i + h]
                mixed.append(dot_nn(vts[i][h * HEAD_DIM:(h + 1) * HEAD_DIM], pbs[2 * i + h]))
            ob[rows_of(i, frames), lanes] = jnp.concatenate(mixed, axis=0).T.astype(BF)
        store(c).start()
        return 0

    lax.fori_loop(0, npair, pair, 0)
    done.append(fetch(ob, ob_o, sem.at[3]))
    p.wait(3)
    accs = [dot_nn(ob[rows_of(i, frames), :], w[3]) for i in range(items)]
    for i, acc in enumerate(accs):
        rr = rows_of(i, frames)
        r1[rr, :] = x[rr, :].astype(F32) + (acc + vec[layer, ROW_OB:ROW_OB + 1, :]) * cms[i]
    done.append(fetch(r1, r1_o, sem.at[4]))

    def finish():
        for c in range(npair):
            store(c).wait()
        for o in done:
            o.wait()

    return finish


def ffn_front(layer, last, items, frames, tab, vec, ub, buf, weights, sems, outs, hooks):
    w_up, w_down, r1, x, n1b, g, gp, acc = buf
    wsem, sem, gsem = sems
    n1b_o, g_o, gp_o, r2_o, out_o = outs
    width, units = w_up.shape
    nch = units // UNIT_CHUNK
    p = Ffn(layer, weights, w_up, w_down, wsem)
    p.start()
    cms = [lane_mask(width, n) for n in tab.w]
    for i in range(items):
        rr = rows_of(i, frames)
        xhat, _ = normed(r1[rr, :], cms[i], tab.inv[i])
        n1 = (xhat * vec[layer, ROW_G1:ROW_G1 + 1, :] + vec[layer, ROW_B1:ROW_B1 + 1, :]) * cms[i]
        n1b[rr, :] = n1.astype(BF)
        acc[rr, :] = n1 + vec[layer, ROW_DB:ROW_DB + 1, :] * cms[i]
    done = [fetch(n1b, n1b_o, sem.at[0])]

    def store(k, c):
        cols = pl.ds(pl.multiple_of(c * UNIT_CHUNK, UNIT_CHUNK), UNIT_CHUNK)
        ref, out = ((g, g_o), (gp, gp_o))[k]
        return pltpu.make_async_copy(ref.at[:, cols], out.at[:, cols], gsem.at[k, c])

    def chunk(c, _):
        for at, hook in hooks.items():
            @pl.when(c == at)
            def _(hook=hook):
                hook()

        p.before(c)
        cols = pl.ds(pl.multiple_of(c * UNIT_CHUNK, UNIT_CHUNK), UNIT_CHUNK)
        ids = lax.broadcasted_iota(jnp.int32, (1, UNIT_CHUNK), 1) + c * UNIT_CHUNK
        us = [dot_nn(n1b[rows_of(i, frames), :], w_up[:, cols]) for i in range(items)]
        gbs = []
        for i, u in enumerate(us):
            fm = (ids < tab.u[i]).astype(F32)
            u = (u + ub[layer, 0:1, cols]) * fm
            half = 0.5 * (1.0 + lax.erf(u * (0.5 ** 0.5)))
            gb = (u * half).astype(BF)
            g[rows_of(i, frames), cols] = gb
            gp[rows_of(i, frames), cols] = ((half + u * (jnp.exp(u * u * -0.5) * 0.3989422804014327)) * fm).astype(BF)
            gbs.append(gb)
        for i, gb in enumerate(gbs):
            acc[rows_of(i, frames), :] += dot_nn(gb, w_down[cols, :]) * cms[i]
        for k in (0, 1):
            store(k, c).start()
        return 0

    lax.fori_loop(0, nch, chunk, 0)
    done.append(fetch(acc, r2_o, sem.at[1]))
    for i in range(items):
        rr = rows_of(i, frames)
        xhat, _ = normed(acc[rr, :], cms[i], tab.inv[i])
        y = ((xhat * vec[layer, ROW_G2:ROW_G2 + 1, :] + vec[layer, ROW_B2:ROW_B2 + 1, :]) * cms[i]).astype(BF)
        if last:
            y = jnp.where(tab.skip[i] == 1, x[rr, :], y)
        x[rr, :] = y
    done.append(fetch(x, out_o, sem.at[2]))

    def finish():
        for c in range(nch):
            for k in (0, 1):
                store(k, c).wait()
        for o in done:
            o.wait()

    return finish


class Quarters:
    def __init__(self, stage, out, sems, first):
        self.stage, self.out, self.sems, self.first = stage, out, sems, first

    def copy(self, y, b):
        return pltpu.make_async_copy(self.stage.at[y, b], self.out.at[y, self.first + b], self.sems.at[y, b])

    def start(self, y, b):
        self.copy(y, b).start()

    def wait(self):
        for y in range(self.stage.shape[0]):
            for b in range(self.stage.shape[1]):
                self.copy(y, b).wait()


def ffn_bwd_kernel(layer, items, frames, last, first, subnet, vec, cot_any, dxn_any, r2_any, r1_any, gp_any, g_any, n1b_any,
                   *rest):
    (da_o, dr1_o, sums, grads, w_up, w_down, cot, dxn, r2, r1, gp, g, n1b, du, df, acc, da, stage, wsem, sem,
     gsem, qsem) = rest[(2 if last else 3):]
    width, units = w_up.shape
    tab = Table(subnet, items, width)
    nblk, nch = units // width, units // UNIT_CHUNK
    loads = [fetch(r2_any, r2, sem.at[0]), fetch(cot_any, cot, sem.at[1])]
    if not last:
        loads.append(fetch(dxn_any, dxn, sem.at[2]))
    p = Ffn(layer, rest[:2], w_up, w_down, wsem)
    p.start()

    def load_gp(c):
        cols = pl.ds(pl.multiple_of(c * UNIT_CHUNK, UNIT_CHUNK), UNIT_CHUNK)
        return pltpu.make_async_copy(gp_any.at[:, cols], gp.at[:, cols], gsem.at[c])

    for c in range(nch):
        load_gp(c).start()
    later = [fetch(r1_any, r1, sem.at[3]), fetch(n1b_any, n1b, sem.at[4]), fetch(g_any, g, sem.at[5])]
    sums[...] = jnp.zeros_like(sums)
    for o in loads:
        o.wait()
    for i in range(items):
        rr = rows_of(i, frames)
        cm = lane_mask(width, tab.w[i])
        if last:
            dy = jnp.where(tab.skip[i] == 1, 0.0, cot[rr, :].astype(F32))
        else:
            dy = jnp.where(tab.skip[i] == 1, cot[rr, :], dxn[rr, :]).astype(F32)
        xhat, rstd = normed(r2[rr, :], cm, tab.inv[i])
        dr2, dg, ds = norm_back(dy, xhat, rstd, vec[ROW_G2:ROW_G2 + 1, :], cm, tab.inv[i])
        dfb = dr2.astype(BF)
        df[rr, :] = dfb
        acc[rr, :] = dr2
        sums[ROW_G2:ROW_G2 + 1, 0:width] += dg
        sums[ROW_B2:ROW_B2 + 1, 0:width] += ds
        sums[ROW_DB:ROW_DB + 1, 0:width] += jnp.sum(dfb.astype(F32), axis=0, keepdims=True)

    def chunk(its, c):
        p.before(c)
        load_gp(c).wait()
        cols = pl.ds(pl.multiple_of(c * UNIT_CHUNK, UNIT_CHUNK), UNIT_CHUNK)
        dgs = [dot_nt(df[rows_of(i, frames), :], w_down[cols, :]) for i in its]
        dubs = []
        for i, dg in zip(its, dgs):
            dub = (dg * gp[rows_of(i, frames), cols].astype(F32)).astype(BF)
            du[rows_of(i, frames), cols] = dub
            sums[ROW_UB:ROW_UB + 1, cols] += jnp.sum(dub.astype(F32), axis=0, keepdims=True)
            dubs.append(dub)
        for i, dub in zip(its, dubs):
            acc[rows_of(i, frames), :] += dot_nt(dub, w_up[:, cols])

    over_both(tab.chunks, chunk)
    p.drain(tab.chunks)

    def drain(c, _):
        load_gp(c).wait()
        return 0

    lax.fori_loop(jnp.maximum(tab.chunks[0], tab.chunks[1]), nch, drain, 0)
    for i in range(items):
        def blank(c, _, i=i):
            cols = pl.ds(pl.multiple_of(c * UNIT_CHUNK, UNIT_CHUNK), UNIT_CHUNK)
            du[rows_of(i, frames), cols] = jnp.zeros((frames, UNIT_CHUNK), BF)
            return 0

        lax.fori_loop(tab.chunks[i], nch, blank, 0)
    for o in later:
        o.wait()
    quarters = Quarters(stage, grads, qsem, first)
    rows = stage.shape[3]

    def down_step(f, _):
        y, par = f // 2, f % 2
        for s in range(nblk // 2):
            lanes = pl.ds(pl.multiple_of(f * width + s * 2 * rows, LANES), 2 * rows)
            res = dot_tn(g[:, lanes], df[...]).astype(BF)
            for t in (0, 1):
                stage[y, 2 * s + t, par] = res[t * rows:(t + 1) * rows]

        @pl.when(par == 1)
        def _():
            for b in range(nblk):
                quarters.start(y, b)
        return 0

    lax.fori_loop(0, 4, down_step, 0)
    for i in range(items):
        rr = rows_of(i, frames)
        cm = lane_mask(width, tab.w[i])
        xhat, rstd = normed(r1[rr, :], cm, tab.inv[i])
        d1, dg, ds = norm_back(acc[rr, :], xhat, rstd, vec[ROW_G1:ROW_G1 + 1, :], cm, tab.inv[i])
        acc[rr, :] = d1
        dab = d1.astype(BF)
        da[rr, :] = dab
        sums[ROW_G1:ROW_G1 + 1, 0:width] += dg
        sums[ROW_B1:ROW_B1 + 1, 0:width] += ds
        sums[ROW_OB:ROW_OB + 1, 0:width] += jnp.sum(dab.astype(F32), axis=0, keepdims=True)
    outs = [fetch(acc, dr1_o, sem.at[6]), fetch(da, da_o, sem.at[7])]

    def up_step(j, _):
        cols = pl.ds(pl.multiple_of(j * width, LANES), width)
        for y in (0, 1):
            res = dot_tn(n1b[:, y * 2 * rows:(y + 1) * 2 * rows], du[:, cols]).astype(BF)
            for t in (0, 1):
                stage[y, nblk + j, t] = res[t * rows:(t + 1) * rows]
            quarters.start(y, nblk + j)
        return 0

    lax.fori_loop(0, nblk, up_step, 0)
    quarters.wait()
    for o in outs:
        o.wait()


ANY = pl.BlockSpec(memory_space=pl.ANY)
VM = pl.BlockSpec(memory_space=pltpu.VMEM)
SM = pl.BlockSpec(memory_space=pltpu.SMEM)
PARAMS = dict(vmem_limit_bytes=58 * 2 ** 20)


def cost(flops, nbytes):
    return pl.CostEstimate(flops=int(flops), bytes_accessed=int(nbytes), transcendentals=0)


def sds(shape, dtype):
    return jax.ShapeDtypeStruct(shape, dtype)


def run(kernel, name, subnet, vmem, hbm, outs, vmem_outs, scratch, sems, flops, nbytes, alias=None):
    return pl.pallas_call(
        kernel,
        out_shape=tuple(outs),
        in_specs=[SM] + [VM] * len(vmem) + [ANY] * len(hbm),
        out_specs=tuple(VM if k in vmem_outs else ANY for k in range(len(outs))),
        scratch_shapes=[pltpu.VMEM(s, d) for s, d in scratch] + [pltpu.SemaphoreType.DMA(s) for s in sems],
        input_output_aliases={} if alias is None else {len(vmem) + len(hbm): alias},
        compiler_params=pltpu.CompilerParams(**PARAMS),
        cost_estimate=cost(flops, nbytes),
        name=name,
    )(subnet, *vmem, *hbm)


def ffn_bwd(layer, last, first, blocks, subnet, cot, dxn, r2, r1, gp, g, n1b, vec, weights, grads, items):
    n, d = cot.shape
    ff = gp.shape[1]
    q, nb = d // 4, ff // d
    more = () if grads is None else (grads,)
    return run(
        functools.partial(ffn_bwd_kernel, layer, items, n // items, last, first), "ffn_bwd", subnet, (vec,),
        (cot, dxn, r2, r1, gp, g, n1b, *weights, *more),
        [sds((n, d), BF), sds((n, d), F32), sds((8, ff), F32), sds((2, blocks, 2, q, d), BF)], (2,),
        [((d, ff), BF), ((ff, d), BF), ((n, d), BF), ((n, d), BF), ((n, d), F32), ((n, d), F32), ((n, ff), BF),
         ((n, ff), BF), ((n, d), BF), ((n, ff), BF), ((n, d), BF), ((n, d), F32), ((n, d), BF),
         ((2, 2 * nb, 2, q, d), BF)],
        [(nb, 2), (8,), (ff // UNIT_CHUNK,), (2, 2 * nb)],
        10 * n * d * ff, 8 * d * ff + n * d * 40, None if grads is None else 3)


MESH = pl.DeviceIdType.MESH


def flip(axis, bit):
    return {axis: jnp.bitwise_xor(lax.axis_index(axis), 1 << bit)}


def greet(partners):
    barrier = pltpu.get_barrier_semaphore()
    for who in partners:
        pl.semaphore_signal(barrier, inc=1, device_id=who, device_id_type=MESH)
    pl.semaphore_wait(barrier, len(partners))


class Gather:
    def __init__(self, layers, shards, full, every, send_sem, recv_sem):
        self.layers, self.shards, self.full, self.every = layers, shards, full, every
        self.send_sem, self.recv_sem = send_sem, recv_sem
        self.f = lax.axis_index("fsdp")
        pipe = lax.axis_index("pipe")
        self.part = 2 * (pipe % 2) + (pipe // 2) % 2
        self.far = jnp.bitwise_xor(self.f, 2)
        self.who = {"c": flip("fsdp", 0), "y": flip("fsdp", 1), "x": flip("pipe", 0), "z": flip("pipe", 1)}
        self.rows, self.width = shards[1].shape[1:]
        self.chunks = [(l, kind) for l in range(layers) for kind in range(3)]
        self.direct = {n: (None, 1, 0)[n % 3] for n in range(len(self.chunks))}
        self.ids, self.began, self.arrived = {}, [], set()

    def at(self, ref, k, layer, row, nrows, col, ncols, quarter):
        base = 0 if quarter is None else pl.multiple_of(quarter * self.shards[k].shape[1], 8)
        return ref.at[layer, pl.ds(pl.multiple_of(base + row, 8), nrows), pl.ds(col, ncols)]

    def place(self, w, l):
        n = self.shards[w].shape[1]
        return self.full[w].at[l, pl.ds(pl.multiple_of(self.f * n, 8), n)]

    def regions(self, n, ab, k):
        kind = self.chunks[n][1]
        d, piece, half = self.width, self.rows // 4, self.rows // 2
        if kind == 0:
            if ab == 0:
                return [(0, piece * k, piece, 0, 2 * d)]
            return [(0, piece * k, piece, 2 * d, d), (1, piece * k, piece, 0, d)]
        row = (kind - 1) * half
        if ab == 0:
            return [(2, row, half, pl.multiple_of(k * d, LANES), d)]
        return [(3, k * self.rows + row, half, 0, d)]

    def copies(self, key):
        kind = key[0]
        if kind == "own":
            _, l, w = key
            pairs, who = [(self.shards[w].at[l], self.place(w, l))], "c"
        elif kind == "small":
            who = key[1]
            row = self.far if key[2] else self.f
            pairs = [(self.every.at[row], self.every.at[row])]
        else:
            _, n, ab, j = key
            l = self.chunks[n][0]
            k = jnp.bitwise_xor(self.part, j)
            who = kind
            pairs = []
            for w, row, nr, col, nc in self.regions(n, ab, k):
                if kind == "y":
                    src = self.at(self.shards[w], w, l, row, nr, col, nc, None)
                    dst = self.at(self.full[w], w, l, row, nr, col, nc, self.f)
                else:
                    src = dst = self.at(self.full[w], w, l, row, nr, col, nc, self.far)
                pairs.append((src, dst))
        out = []
        for m, (src, dst) in enumerate(pairs):
            sem = self.ids.setdefault((key, m), len(self.ids))
            out.append(pltpu.make_async_remote_copy(
                src_ref=src, dst_ref=dst, send_sem=self.send_sem.at[sem], recv_sem=self.recv_sem.at[sem],
                device_id=self.who[who], device_id_type=MESH))
        return out

    def start(self, *key):
        for c in self.copies(key):
            c.start()
        self.began.append(key)

    def landed(self, *key):
        if key not in self.arrived:
            for c in self.copies(key):
                c.wait_recv()
            self.arrived.add(key)

    def tick(self, t):
        count = len(self.chunks)
        if t < count:
            for ab in (0, 1):
                self.start("y", t, ab, 0)
            if self.direct[t] is not None:
                self.start("y", t, self.direct[t], 3)
        n = t - 3
        if 0 <= n < count:
            self.landed("x", n, 1, 0)
            self.landed("z", n, 0, 0)
            self.start("c", n, 1, 2)
            self.start("c", n, 0, 1)
            for ab, link in ((0, "z"), (1, "x")):
                if self.direct[n] != ab:
                    self.landed(link, n, ab, 2 if ab == 0 else 1)
                    self.start("c", n, ab, 3)
        n = t - 2
        if 0 <= n < count:
            self.landed("x", n, 0, 0)
            self.landed("z", n, 1, 0)
            if self.direct[n] != 0:
                self.start("z", n, 0, 2)
            if self.direct[n] != 1:
                self.start("x", n, 1, 1)
            if self.direct[n] is not None:
                self.landed("y", n, self.direct[n], 3)
                self.start("c", n, self.direct[n], 3)
            self.start("c", n, 0, 2)
            self.start("c", n, 1, 1)
        n = t - 1
        if 0 <= n < count:
            for ab in (0, 1):
                self.landed("y", n, ab, 0)
            for ab in (0, 1):
                self.start("x", n, ab, 0)
                self.start("z", n, ab, 0)
            for ab in (0, 1):
                self.start("c", n, ab, 0)

    def ready(self, n):
        for ab in (0, 1):
            for j in range(4):
                self.landed("c", n, ab, j)

    def drain(self):
        for key in self.began:
            for c in self.copies(key):
                c.wait_send()


def fore_kernel(layers, items, frames, subnet, *rest):
    smalls, (x_any, *shards) = rest[:8], rest[8:13]
    outs = rest[13:]
    full, (vec, ub, x1_o, out_o) = outs[:4], outs[4:8]
    kept = [outs[8 + 8 * l:16 + 8 * l] for l in range(layers)]
    scratch = outs[8 + 8 * layers:]
    every, own, (send_sem, recv_sem, local_sem) = scratch[0], scratch[1:5], scratch[5:8]
    w, x, qkv, pt, ob, r1, w_up, w_down, n1b, g, gp, acc = scratch[8:20]
    asem, fsem, xsem = scratch[20:23], scratch[23:26], scratch[26]
    width = x.shape[1]
    tab = Table(subnet, items, width)
    gat = Gather(layers, shards, full, every, send_sem, recv_sem)
    order = [(k, l) for l in range(layers) for k in range(4)]
    loads = [pltpu.make_async_copy(shards[k].at[l], own[k].at[l], local_sem.at[0, k, l]) for k, l in order]
    stores = [pltpu.make_async_copy(own[k].at[l], gat.place(k, l), local_sem.at[1, k, l]) for k, l in order]
    load_x = fetch(x_any, x, xsem.at[0])
    for c in loads:
        c.start()
    every[gat.f] = jnp.zeros(every.shape[1:], F32)
    for k, ref in enumerate(smalls):
        for l in range(layers):
            every[gat.f, l, k:k + 1, 0:ref.shape[1]] = ref[l:l + 1, :].astype(F32)
    greet(list(gat.who.values()))
    gat.start("small", "y", 0)
    gat.start("small", "c", 0)
    gat.tick(0)
    for c, d in zip(loads, stores):
        c.wait()
        d.start()
    gat.landed("small", "y", 0)
    gat.start("small", "c", 1)
    for k in range(4):
        gat.start("own", 0, k)
    load_x.wait()
    mask_rows(x, items, frames, tab)
    for t in (1, 2, 3):
        gat.tick(t)
    gat.landed("small", "c", 0)
    gat.landed("small", "c", 1)
    rows = gat.rows
    for q in range(4):
        for l in range(layers):
            vec[l, 0:7, q * rows:(q + 1) * rows] = every[q, l, 0:7, 0:rows]
            ub[l, :, q * width:(q + 1) * width] = every[q, l, 7:8, :]
    for c in stores:
        c.wait()
    for l in range(1, layers):
        for k in range(4):
            gat.start("own", l, k)

    last_tick = len(gat.chunks) + 2
    state = [4]

    def tick_to(t):
        while state[0] <= min(t, last_tick):
            gat.tick(state[0])
            state[0] += 1

    def hook_for(t):
        def hook():
            gat.tick(t)
        return hook

    def reserve():
        if state[0] > last_tick:
            return {}
        t = state[0]
        state[0] += 1
        return {3: hook_for(t)}

    pending = None
    for l in range(layers):
        tick_to(3 * l + 3)
        for k in (0, 1):
            gat.landed("own", l, k)
        gat.ready(3 * l)
        if pending is not None:
            pending[0]()
        hooks = reserve()
        end_a = attn_front(
            l, items, frames, tab, vec, (w, x, qkv, pt, ob, r1), full[:2], asem, kept[l][:4], hooks)
        tick_to(3 * l + 5)
        for k in (2, 3):
            gat.landed("own", l, k)
        gat.ready(3 * l + 1)
        gat.ready(3 * l + 2)
        if pending is not None:
            pending[1]()
        last = l == layers - 1
        hooks = reserve()
        end_f = ffn_front(
            l, last, items, frames, tab, vec, ub, (w_up, w_down, r1, x, n1b, g, gp, acc), full[2:], fsem,
            (*kept[l][4:], out_o if last else x1_o), hooks)
        pending = (end_a, end_f)
    pending[0]()
    pending[1]()
    gat.drain()


def fore(subnet, smalls, x, weights):
    layers = weights[0].shape[0]
    items, t, d = x.shape
    n = items * t
    ff = weights[2].shape[2]
    vm, dma = pltpu.VMEM, pltpu.SemaphoreType.DMA
    keep = [sds((3, n, d), BF), sds((items, HEADS, t, t), BF), sds((n, d), BF), sds((n, d), F32), sds((n, d), BF),
            sds((n, ff), BF), sds((n, ff), BF), sds((n, d), F32)]
    outs = [sds((layers, 4 * w.shape[1], w.shape[2]), BF) for w in weights] + [
        sds((layers, 8, d), F32), sds((layers, 1, ff), F32), sds((n, d), BF), sds((n, d), BF)] + keep * layers
    square = vm((n, d), BF)
    res = pl.pallas_call(
        functools.partial(fore_kernel, layers, items, t),
        out_shape=tuple(outs),
        in_specs=[SM] + [VM] * 8 + [ANY] * 5,
        out_specs=tuple(VM if k in (4, 5) else ANY for k in range(len(outs))),
        scratch_shapes=[
            vm((4, layers, 8, d), F32), *[vm(w.shape, BF) for w in weights], dma((200,)), dma((200,)), dma((2, 4, layers)),
            vm((4, d, d), BF), square, vm((3, n, d), BF), vm((items, HEADS, t, t), BF), square, vm((n, d), F32),
            vm((d, ff), BF), vm((ff, d), BF), square, vm((n, ff), BF), vm((n, ff), BF), vm((n, d), F32),
            dma((4,)), dma((5,)), dma((d // LANES,)), dma((ff // d, 2)), dma((3,)), dma((2, ff // UNIT_CHUNK)), dma((1,)),
        ],
        compiler_params=pltpu.CompilerParams(collective_id=0, has_side_effects=True, vmem_limit_bytes=60 * 2 ** 20),
        name="fore",
    )(subnet, *smalls, x.reshape(n, d), *weights)
    return res[:4], res[4], res[5], res[6], res[7], [res[8 + 8 * l:16 + 8 * l] for l in range(layers)]


class Reduce:
    LOC, RECV = 6, 4

    def __init__(self, count, bits, g, out, refs):
        self.count, self.bits, self.g, self.out = count, bits, g, out
        self.loc, self.rc, self.ry, self.rx, self.rz, self.fin, self.ss, self.rs, self.ls, self.os = refs
        f, pipe = lax.axis_index("fsdp"), lax.axis_index("pipe")
        self.c, self.y, x, z = f % 2, f // 2, pipe % 2, (pipe // 2) % 2
        rows = g.shape[3]
        half, quarter = rows // 2, rows // 4
        self.who = [flip("fsdp", 0), flip("fsdp", 1)] + [flip("pipe", b) for b in range(bits)]
        part = lambda at, n: pl.ds(pl.multiple_of(at, 16), n)
        self.my_half, self.their_half = part(x * half, half), part((1 - x) * half, half)
        self.mine, self.theirs = part(x * half + z * quarter, quarter), part(x * half + (1 - z) * quarter, quarter)
        self.n_red = 2 + bits
        self.total = self.n_red + 2
        self.slots = self.fin.shape[0]

    @staticmethod
    def scratch(bits, count, rows, d):
        vm, dma = pltpu.VMEM, pltpu.SemaphoreType.DMA
        n = bits + 4
        return [
            vm((Reduce.LOC, 2, rows, d), BF), vm((Reduce.RECV, 2, rows, d), BF), vm((Reduce.RECV, rows, d), BF),
            vm((Reduce.RECV, rows // 2, d), BF), vm((bits - 1, Reduce.RECV, rows // 4, d), BF), vm((n + 2, rows, d), BF),
            dma((n, count)), dma((n, count)), dma((count,)), dma((count,)),
        ]

    def load(self, p):
        return pltpu.make_async_copy(self.g.at[:, p, self.c], self.loc.at[p % self.LOC], self.ls.at[p])

    def store(self, p):
        return pltpu.make_async_copy(self.fin.at[p % self.slots], self.out.at[p], self.os.at[p])

    def move(self, k, p):
        loc, fin, r = self.loc.at[p % self.LOC], self.fin.at[p % self.slots], p % self.RECV
        if k == 0:
            src, dst, who = self.g.at[:, p, 1 - self.c], self.rc.at[r], 0
        elif k == 1:
            src, dst, who = loc.at[1 - self.y], self.ry.at[r], 1
        elif k == 2:
            src, dst, who = loc.at[self.y, self.their_half], self.rx.at[r], 2
        elif k == 3:
            src, dst, who = loc.at[self.y, self.theirs], self.rz.at[0, r], 3
        elif k < self.n_red:
            src, dst, who = fin.at[self.mine], self.rz.at[k - 3, r], k
        elif k == self.n_red:
            src, dst, who = fin.at[self.mine], fin.at[self.mine], 3
        else:
            src, dst, who = fin.at[self.my_half], fin.at[self.my_half], 2
        return pltpu.make_async_remote_copy(
            src_ref=src, dst_ref=dst, send_sem=self.ss.at[k, p], recv_sem=self.rs.at[k, p], device_id=self.who[who],
            device_id_type=MESH)

    def arrive(self, k, p):
        self.move(k, p).wait()
        s, f, r = p % self.LOC, p % self.slots, p % self.RECV
        if k == 0:
            self.load(p).wait()
            self.loc[s] = add_low(self.loc[s], self.rc[r])
        elif k == 1:
            self.loc[s, self.y] = add_low(self.loc[s, self.y], self.ry[r])
        elif k == 2:
            self.loc[s, self.y, self.my_half] = add_low(self.loc[s, self.y, self.my_half], self.rx[r])
        elif k == 3:
            self.fin[f, self.mine] = add_low(self.loc[s, self.y, self.mine], self.rz[0, r])
        elif k < self.n_red:
            self.fin[f, self.mine] = add_low(self.fin[f, self.mine], self.rz[k - 3, r])

    def begin(self):
        self.move(0, 0).start()
        self.load(0).start()

    def tick(self, t):
        @pl.when(t + 1 < self.count)
        def _():
            self.move(0, t + 1).start()
            self.load(t + 1).start()

        for k in range(self.total):
            p = t - k

            @pl.when(jnp.logical_and(p >= 0, p < self.count))
            def _(k=k, p=p):
                self.arrive(k, p)
                if k + 1 < self.total:
                    self.move(k + 1, p).start()
                else:
                    self.store(p).start()

        p = t - self.total

        @pl.when(jnp.logical_and(p >= 0, p < self.count))
        def _():
            self.store(p).wait()

    def ticks(self):
        return self.count + self.total


def add_low(a, b):
    return (a.astype(F32) + b.astype(F32)).astype(BF)


class SumAll:
    def __init__(self, who, total, recv, ss, rs):
        self.who, self.total, self.recv, self.ss, self.rs = who, total, recv, ss, rs

    def move(self, k):
        return pltpu.make_async_remote_copy(
            src_ref=self.total, dst_ref=self.recv.at[k], send_sem=self.ss.at[k], recv_sem=self.rs.at[k],
            device_id=self.who[k], device_id_type=MESH)

    def step(self, k):
        for j in range(len(self.who) + 1):
            @pl.when(k == j)
            def _(j=j):
                if j > 0:
                    self.move(j - 1).wait()
                    self.total[...] = self.total[...] + self.recv[j - 1]
                if j < len(self.who):
                    self.move(j).start()


def attn_back(layer, items, frames, tab, src, buf, weights, sems, first, grads, tick, t0, dx_out):
    qkv_any, pt_any, x_any, ob_any = src
    w, da, dr1, qkv, pt, x, ob, do, dqkv, dx, stage = buf
    wsem, sem, ptsem, qsem = sems
    width = da.shape[1]
    npair = width // LANES
    ring = pt.shape[0]
    p = Attn(layer, weights, w, wsem)
    p.start((3, 0, 1, 2))

    def block(ref, j):
        return ref.at[:, pl.ds(pl.multiple_of(j * width, LANES), width)]

    loads = [fetch(qkv_any.at[j], block(qkv, j), sem.at[3 + j]) for j in range(3)]

    def load_pt(c):
        return pltpu.make_async_copy(pt_any.at[:, pl.ds(2 * c, 2)], pt.at[c % ring], ptsem.at[c])

    for c in range(ring - 1):
        load_pt(c).start()
    later = [fetch(ob_any, ob, sem.at[0]), fetch(x_any, x, sem.at[1])]
    p.wait(3)
    dos = [dot_nt(da[rows_of(i, frames), :], w[3]) for i in range(items)]
    for i, d in enumerate(dos):
        do[rows_of(i, frames), :] = d.astype(BF)
    for o in loads:
        o.wait()
    scale = HEAD_DIM ** -0.5
    qsums = []

    def pair(c, _):
        @pl.when(c % 3 == 0)
        def _():
            tick(t0 + c // 3)

        lanes = pl.ds(pl.multiple_of(c * LANES, LANES), LANES)
        ids = lax.broadcasted_iota(jnp.int32, (1, LANES), 1) + c * LANES
        load_pt(c).wait()

        @pl.when(c + ring - 1 < npair)
        def _():
            load_pt(c + ring - 1).start()

        rr = [rows_of(i, frames) for i in range(items)]
        at = [pl.ds(pl.multiple_of(j * width + c * LANES, LANES), LANES) for j in range(3)]
        q = [qkv[r, at[0]] for r in rr]
        k = [qkv[r, at[1]] for r in rr]
        v = [qkv[r, at[2]] for r in rr]
        dob = [do[r, lanes] for r in rr]
        kt = [a.T for a in k]
        heads = [(n, h) for n in range(items) for h in (0, 1)]
        pbs = [pt[c % ring, n, h] for n, h in heads]
        dps = [dot_nt(only(h, v[n]), dob[n]) for n, h in heads]
        dvs = [dot_nn(pb, dob[n]) for pb, (n, h) in zip(pbs, heads)]
        tmps = [pb.astype(F32) * dp for pb, dp in zip(pbs, dps)]
        dss = [(t - pb.astype(F32) * jnp.sum(t, axis=0, keepdims=True)).astype(BF) for t, pb in zip(tmps, pbs)]
        dks = [dot_nn(ds, q[n]) for ds, (n, h) in zip(dss, heads)]
        dqs = [dot_nn(kt[n][h * HEAD_DIM:(h + 1) * HEAD_DIM], ds) for ds, (n, h) in zip(dss, heads)]
        for n in range(items):
            on = ids < tab.a[n]
            put = lambda v, s: jnp.where(on, v * s, 0.0).astype(BF)
            dqkv[rr[n], at[0]] = put(jnp.concatenate(dqs[2 * n:2 * n + 2], axis=0).T, scale)
            dqkv[rr[n], at[1]] = put(jnp.where(half_mask(0), dks[2 * n], dks[2 * n + 1]), scale)
            dqkv[rr[n], at[2]] = put(jnp.where(half_mask(0), dvs[2 * n], dvs[2 * n + 1]), 1.0)
        return 0

    lax.fori_loop(0, npair, pair, 0)
    t0 = t0 + (npair + 2) // 3
    tick(t0)
    q_sum = jnp.sum(dqkv[:, 0:width].astype(F32), axis=0, keepdims=True)
    for o in later:
        o.wait()
    if layer == 0:
        mask_rows(x, items, frames, tab)
    quarters = Quarters(stage, grads, qsem, first)
    rows = stage.shape[3]

    def step(lhs, rhs, b):
        for y in (0, 1):
            res = dot_tn(lhs[:, y * 2 * rows:(y + 1) * 2 * rows], rhs).astype(BF)
            for t in (0, 1):
                stage[y, b, t] = res[t * rows:(t + 1) * rows]
            quarters.start(y, b)

    def in_step(j, _):
        step(x, block(dqkv, j)[...], j)
        return 0

    lax.fori_loop(0, 3, in_step, 0)
    tick(t0 + 1)
    step(ob, da[...], 3)
    for j in range(3):
        p.wait(j)

    def back_step(j, _):
        adds = [dot_nt(block(dqkv, j)[rows_of(i, frames), :], w[j]) for i in range(items)]
        for i, add in enumerate(adds):
            dr1[rows_of(i, frames), :] += add
        return 0

    lax.fori_loop(0, 3, back_step, 0)
    for i in range(items):
        rr = rows_of(i, frames)
        dx[rr, :] = (dr1[rr, :] * lane_mask(width, tab.w[i])).astype(BF)
    if dx_out is not None:
        fetch(dx, dx_out, sem.at[2])
    quarters.wait()
    tick(t0 + 2)
    return t0 + 3, q_sum


def ffn_back(layer, items, frames, tab, vec, src, buf, weights, sems, first, grads, tick, t0, sums):
    cot_any, r2_any, r1_any, gp_any, g_any, n1b_any = src
    w_up, w_down, cot, dxn, r, du, g, n1b, df, acc, da, stage = buf
    wsem, sem, gsem, qsem = sems
    width, units = w_up.shape
    nblk, nch = units // width, units // UNIT_CHUNK
    p = Ffn(layer, weights, w_up, w_down, wsem)
    p.start()
    loads = [fetch(r2_any, r, sem.at[0]), fetch(cot_any, cot, sem.at[1])]

    def load_gp(c):
        cols = pl.ds(pl.multiple_of(c * UNIT_CHUNK, UNIT_CHUNK), UNIT_CHUNK)
        return pltpu.make_async_copy(gp_any.at[:, cols], du.at[:, cols], gsem.at[c])

    for c in range(nch):
        load_gp(c).start()
    later = [fetch(n1b_any, n1b, sem.at[3]), fetch(g_any, g, sem.at[4])]
    for o in loads:
        o.wait()
    for i in range(items):
        rr = rows_of(i, frames)
        cm = lane_mask(width, tab.w[i])
        dy = jnp.where(tab.skip[i] == 1, cot[rr, :], dxn[rr, :]).astype(F32)
        xhat, rstd = normed(r[rr, :], cm, tab.inv[i])
        dr2, dg, ds = norm_back(dy, xhat, rstd, vec[layer, ROW_G2:ROW_G2 + 1, :], cm, tab.inv[i])
        dfb = dr2.astype(BF)
        df[rr, :] = dfb
        acc[rr, :] = dr2
        sums[ROW_G2:ROW_G2 + 1, 0:width] += dg
        sums[ROW_B2:ROW_B2 + 1, 0:width] += ds
        sums[ROW_DB:ROW_DB + 1, 0:width] += jnp.sum(dfb.astype(F32), axis=0, keepdims=True)
    load_r1 = fetch(r1_any, r, sem.at[2])
    tick(t0)

    def chunk(c):
        p.before(c)
        load_gp(c).wait()
        cols = pl.ds(pl.multiple_of(c * UNIT_CHUNK, UNIT_CHUNK), UNIT_CHUNK)
        dgs = [dot_nt(df[rows_of(i, frames), :], w_down[cols, :]) for i in range(items)]
        dubs = []
        for i, dg in enumerate(dgs):
            dub = (dg * du[rows_of(i, frames), cols].astype(F32)).astype(BF)
            du[rows_of(i, frames), cols] = dub
            sums[ROW_UB:ROW_UB + 1, cols] += jnp.sum(dub.astype(F32), axis=0, keepdims=True)
            dubs.append(dub)
        for i, dub in enumerate(dubs):
            acc[rows_of(i, frames), :] += dot_nt(dub, w_up[:, cols])

    def one(c, _):
        @pl.when(jnp.logical_and(c % 3 == 0, c > 0))
        def _():
            tick(t0 + c // 3)

        chunk(c)
        return 0

    lax.fori_loop(0, nch, one, 0)
    t0 = t0 + (nch + 2) // 3
    tick(t0)
    for o in later:
        o.wait()
    rows = stage.shape[3]
    down = Quarters(stage, grads, qsem.at[0], first)
    up = Quarters(stage, grads, qsem.at[1], first + nblk)

    def down_step(f, _):
        y, par = f // 2, f % 2
        for s in range(nblk // 2):
            lanes = pl.ds(pl.multiple_of(f * width + s * 2 * rows, LANES), 2 * rows)
            res = dot_tn(g[:, lanes], df[...]).astype(BF)
            for t in (0, 1):
                stage[y, 2 * s + t, par] = res[t * rows:(t + 1) * rows]
        return 0

    lax.fori_loop(0, 4, down_step, 0)
    for y in (0, 1):
        for b in range(nblk):
            down.start(y, b)
    tick(t0 + 1)
    load_r1.wait()
    for i in range(items):
        rr = rows_of(i, frames)
        cm = lane_mask(width, tab.w[i])
        xhat, rstd = normed(r[rr, :], cm, tab.inv[i])
        d1, dg, ds = norm_back(acc[rr, :], xhat, rstd, vec[layer, ROW_G1:ROW_G1 + 1, :], cm, tab.inv[i])
        acc[rr, :] = d1
        dab = d1.astype(BF)
        da[rr, :] = dab
        sums[ROW_G1:ROW_G1 + 1, 0:width] += dg
        sums[ROW_B1:ROW_B1 + 1, 0:width] += ds
        sums[ROW_OB:ROW_OB + 1, 0:width] += jnp.sum(dab.astype(F32), axis=0, keepdims=True)
    down.wait()
    tick(t0 + 2)

    def up_step(j, _):
        cols = pl.ds(pl.multiple_of(j * width, LANES), width)
        for y in (0, 1):
            res = dot_tn(n1b[:, y * 2 * rows:(y + 1) * 2 * rows], du[:, cols]).astype(BF)
            for t in (0, 1):
                stage[y, j, t] = res[t * rows:(t + 1) * rows]
            up.start(y, j)
        return 0

    lax.fori_loop(0, nblk, up_step, 0)
    up.wait()
    tick(t0 + 3)
    return t0 + 4


def back_kernel(items, frames, bits, blocks, subnet, vec, s_top, da_any, dr1_any, cot_any, *rest):
    top, bottom, mid, weights = rest[:4], rest[4:8], rest[8:13], rest[13:17]
    (dx_o, grads, out, total, w_up, w, da, dr1, pt, x, ob, do, dx, r, du, g, stage, srecv) = rest[18:36]
    asem, bsem, fsem = rest[36:40], rest[40:44], rest[44:48]
    red = Reduce(2 * blocks, bits, grads, out, rest[48:58])
    s_send, s_recv, isem = rest[58:]
    width = da.shape[1]
    tab = Table(subnet, items, width)
    loads = [fetch(da_any, da, isem.at[0]), fetch(dr1_any, dr1, isem.at[1])]
    greet(red.who)
    red.begin()
    total[1] = s_top[...]
    total[0] = jnp.zeros(total.shape[1:], F32)
    nb = w_up.shape[1] // width
    w_att, w_ffn = weights[:2], weights[2:]
    for o in loads:
        o.wait()
    buf = (w, da, dr1, du, pt, x, ob, do, g, dx, stage)
    t, q_sum = attn_back(1, items, frames, tab, top, buf, w_att, asem, 2 * nb, grads, red.tick, 0, None)
    total[1, ROW_QB:ROW_QB + 1, 0:width] = q_sum
    w_down = w.reshape(nb * width, width)
    buf_f = (w_up, w_down, x, dx, r, du, g, ob, do, dr1, da, stage)
    t = ffn_back(0, items, frames, tab, vec, (cot_any,) + tuple(mid), buf_f, w_ffn, fsem, blocks, grads, red.tick, t, total.at[0])
    t, q_sum = attn_back(0, items, frames, tab, bottom, buf, w_att, bsem, blocks + 2 * nb, grads, red.tick, t, dx_o)
    total[0, ROW_QB:ROW_QB + 1, 0:width] = q_sum
    small = SumAll(red.who, total, srecv, s_send, s_recv)

    def rest_of(n, _):
        red.tick(n)
        small.step(n - t)
        return 0

    lax.fori_loop(t, red.ticks(), rest_of, 0)
    pltpu.make_async_copy(dx, dx_o, bsem[1].at[2]).wait()


def back(subnet, vec, s_top, da, dr1, cot, top, bottom, mid, weights, grads, items):
    bits = 0
    while (1 << bits) < lax.axis_size("pipe"):
        bits += 1
    n, d = cot.shape
    ff = mid[2].shape[1]
    t = n // items
    rows, nb = d // 4, ff // d
    blocks = 2 * nb + 4
    small = (2,) + s_top.shape
    vm, dma = pltpu.VMEM, pltpu.SemaphoreType.DMA
    square = vm((n, d), BF)
    hbm = (da, dr1, cot, *top, *bottom, *mid, *weights, grads)
    asems = [dma((4,)), dma((6,)), dma((d // LANES,)), dma((2, 4))]
    return pl.pallas_call(
        functools.partial(back_kernel, items, t, bits, blocks),
        out_shape=(sds((n, d), BF), sds(grads.shape, BF), sds((2 * blocks, rows, d), BF), sds(small, F32)),
        in_specs=[SM, VM, VM] + [ANY] * len(hbm),
        out_specs=(ANY, ANY, ANY, VM),
        scratch_shapes=[
            vm((d, ff), BF), vm((4, d, d), BF), square, vm((n, d), F32), vm((3, items, 2, t, t), BF),
            square, square, square, square, vm((n, d), F32), vm((n, ff), BF), vm((n, ff), BF),
            vm((2, 4, 2, rows, d), BF), vm((2 + bits,) + small, F32),
            *asems, *asems, dma((nb, 2)), dma((5,)), dma((ff // UNIT_CHUNK,)), dma((2, 2, nb)),
            *Reduce.scratch(bits, 2 * blocks, rows, d), dma((2 + bits,)), dma((2 + bits,)), dma((2,)),
        ],
        input_output_aliases={2 + len(hbm): 1},
        compiler_params=pltpu.CompilerParams(collective_id=1, has_side_effects=True, vmem_limit_bytes=60 * 2 ** 20),
        name="back",
    )(subnet, vec, s_top, *hbm)


def finish_kernel(layers, red, total, g_in, g_out, g_up, g_down, *rest):
    vecs, (bf, f32, sem_in, sem_out) = rest[:8], rest[8:]
    f = lax.axis_index("fsdp")
    blocks = bf.shape[0]
    rows, d = bf.shape[1:]
    per = blocks // layers
    nb = (per - 4) // 2

    def target(l, k):
        if k < nb:
            return g_down.at[l, pl.ds(k * rows, rows)]
        if k < 2 * nb:
            return g_up.at[l, :, pl.ds((k - nb) * d, d)]
        if k < 2 * nb + 3:
            return g_in.at[l, :, pl.ds((k - 2 * nb) * d, d)]
        return g_out.at[l]

    loads = [pltpu.make_async_copy(red.at[p], bf.at[p], sem_in.at[p]) for p in range(blocks)]
    stores = [pltpu.make_async_copy(f32.at[p], target(layers - 1 - p // per, p % per), sem_out.at[p]) for p in range(blocks)]
    for c in loads:
        c.start()
    for q in range(4):
        @pl.when(f == q)
        def _(q=q):
            for l in range(layers):
                for k in range(7):
                    vecs[k][l:l + 1, :] = total[l, k:k + 1, q * rows:(q + 1) * rows]
                vecs[7][l:l + 1, :] = total[l, 7:8, q * d:(q + 1) * d]
    for p in range(blocks):
        loads[p].wait()
        f32[p] = bf[p].astype(F32)
        stores[p].start()
    for c in stores:
        c.wait()


def finish(red, total):
    blocks, rows, d = red.shape
    layers = total.shape[0]
    nb = (blocks // layers - 4) // 2
    return pl.pallas_call(
        functools.partial(finish_kernel, layers),
        out_shape=(sds((layers, rows, 3 * d), F32), sds((layers, rows, d), F32), sds((layers, rows, nb * d), F32),
                   sds((layers, nb * rows, d), F32)) + (sds((layers, rows), F32),) * 7 + (sds((layers, d), F32),),
        in_specs=[ANY, VM],
        out_specs=(ANY,) * 4 + (VM,) * 8,
        scratch_shapes=[pltpu.VMEM(red.shape, BF), pltpu.VMEM(red.shape, F32), pltpu.SemaphoreType.DMA((blocks,)),
                        pltpu.SemaphoreType.DMA((blocks,))],
        compiler_params=pltpu.CompilerParams(**PARAMS),
        name="finish",
    )(red, total)


def local(
    frames_in, attn_in, q_bias, attn_out, out_bias, norm1_gain, norm1_bias, ffn_up, up_bias, ffn_down, down_bias,
    norm2_gain, norm2_bias, subnet, out_cotangent,
):
    items, frames, width = frames_in.shape
    ff = ffn_up.shape[2]
    layers = attn_in.shape[0]
    nb = ff // width
    smalls = (q_bias, out_bias, norm1_gain, norm1_bias, down_bias, norm2_gain, norm2_bias, up_bias)
    n = items * frames
    weights, vec, ub, x1, layer_out, kept = fore(subnet, smalls, frames_in, (attn_in, attn_out, ffn_up, ffn_down))
    layer_out = layer_out.reshape(frames_in.shape)
    cot = out_cotangent.reshape(n, width)
    qkv1, pt1, ob1, r1, n1b, g, gp, r2 = kept[1]
    da, dr1, s_top, grads = ffn_bwd(
        1, True, 0, 2 * (2 * nb + 4), subnet, cot, cot, r2, r1, gp, g, n1b, vec[1], weights[2:], None, items)
    x0 = frames_in.reshape(n, width)
    qkv0, pt0, ob0, r1, n1b, g, gp, r2 = kept[0]
    dx, _, red, total = back(
        subnet, vec, s_top, da, dr1, cot, (qkv1, pt1, x1, ob1), (qkv0, pt0, x0, ob0), (r2, r1, gp, g, n1b), weights, grads,
        items)
    dx = dx.reshape(frames_in.shape)
    g_in, g_out, g_up, g_down, g_qb, g_ob, g_g1, g_b1, g_db, g_g2, g_b2, g_ub = finish(red, total)
    return (layer_out, dx, g_in, g_qb, g_out, g_ob, g_g1, g_b1, g_up, g_ub, g_down, g_db, g_g2, g_b2)


def solution(mesh):
    rows3 = P(None, "fsdp", None)
    rows2 = P(None, "fsdp")
    item = P(("pipe", "fsdp"), None, None)
    weights = (rows3, rows2, rows3, rows2, rows2, rows2, rows3, rows2, rows3, rows2, rows2, rows2)
    return jax.shard_map(
        local, mesh=mesh, in_specs=(item,) + weights + (P(), item), out_specs=(item, item) + weights, check_vma=False,
    )
```

profile of v0, /device:TPU:0, one launch (start us, length us, event | category | flops | bytes accessed | tf_op | source)
XLA Modules:
  0.0 343.4 jit_solution(9419169044159192674)
XLA Ops:
  0.7 97.9 %fore.1 = (bf16[2,768,2304]{2,1,0:T(8,128)(2,1)}, bf16[2,768,768]{2,1,0:T(8,128)(2,1)}, bf16[2,768,3072]{2,1,0:T(8,128)(2,1)}, bf16[2,3072,768]{2,1,0:T(8,128)(2...) custom-call(s32[4,4]{1,0:T(4,128)} %subnet.5, ...), custom_call_target="tpu_custom_call" | custom-call | tf_op jit(solution)/shard_map/fore/pallas_call | solution.py:727
  98.6 1.3 slice_bitcast_fusion.vec
  99.9 28.1 %ffn_bwd.1 = (bf16[768,768]{1,0:T(8,128)(2,1)}, f32[768,768]{1,0:T(8,128)}, f32[8,3072]{1,0:T(8,128)}, bf16[2,24,2,192,768]{4,3,2,1,0:T(8,128)(2,1)}) custom-call(s32[4,4]{1,0:T(4,128)} %subnet.5, f32[8,768]{1,0:T(8,128)} %slice_bitcast_fusion.vec, bf16[768,768]{1,0:T(8,128)(2,1)} %bitcast.10, bf16[768,768]{1,0:T(8,128)(2,1)} %bitcast.11, ...), custom_call_target="tpu_custom_call" | custom-call | flops 18119393280 | bytes 42467328 | tf_op jit(solution)/shard_map/ffn_bwd/pallas_call | solution.py:448
  128.0 203.6 %back.1 = (bf16[768,768]{1,0:T(8,128)(2,1)}, bf16[2,24,2,192,768]{4,3,2,1,0:T(8,128)(2,1)}, bf16[24,192,768]{2,1,0:T(8,128)(2,1)}, f32[2,8,3072]{2,1,0:T(8,128)}) custom-call(s32[4,4]{1,0:T(4,128)} %subnet.5, f32[2,8,768]{2,1,0:T(8,128)} %get-tuple-element.57.vec, f32[8,3072]{1,0:T(8,128)} %get-tuple-element.65.s_top, ...), custom_call_target="tpu_custom_call", output_to_operand_aliasing={{1}: (23, {})} | custom-call | tf_op jit(solution)/shard_map/back/pallas_call | solution.py:1138
  331.6 0.0 copy-start
  331.7 8.8 %finish.1 = (f32[2,192,2304]{2,1,0:T(8,128)}, f32[2,192,768]{2,1,0:T(8,128)}, f32[2,192,3072]{2,1,0:T(8,128)}, f32[2,768,768]{2,1,0:T(8,128)}, f32[2,192]{1,0:T(...) custom-call(bf16[24,192,768]{2,1,0:T(8,128)(2,1)} %get-tuple-element, ...), custom_call_target="tpu_custom_call" | custom-call | tf_op jit(solution)/shard_map/finish/pallas_call | solution.py:1196
  340.5 0.0 copy-start.1
  340.5 0.0 copy-done
  340.5 1.0 copy.33
  341.5 0.7 copy-done.1
  342.2 1.0 copy.34
Async XLA Ops:
  331.6 8.8 %copy-start = (bf16[768,768]{1,0:T(8,128)(2,1)S(1)}, bf16[768,768]{1,0:T(8,128)(2,1)}, u32[]{:S(2)}) copy-start(bf16[768,768]{1,0:T(8,128)(2,1)} %get-tuple-element.56) | copy-start | bytes 3538948
  340.5 1.7 copy-start.1
where the time goes:
time: 346 us; the launch traced here: 343 us
  Pallas kernels  338 us (98%)
  local copies, waits for them, and re-layouts  4.04 us (1%)
    pallas_call x1, Pallas kernels, back(): pl.pallas_call(functools.partial(back_kernel, items, t, bits, blocks), ou...  204 us
    pallas_call x1, Pallas kernels, fore(): pl.pallas_call(functools.partial(fore_kernel, layers, items, t), out_shap...  97.9 us
    pallas_call x1, Pallas kernels, run(): pl.pallas_call(kernel, out_shape=tuple(outs), in_specs=[SM] + [VM] * len(...  28.1 us
    pallas_call x1, Pallas kernels, finish(): pl.pallas_call(functools.partial(finish_kernel, layers), out_shape=(sds((...  8.81 us

commit v1 on v0

--- a/solution.py
+++ b/solution.py
@@ -122,31 +122,10 @@
     return copy
 
 
-def pick(i, values):
-    return values[i] if isinstance(i, int) else jnp.where(i == 0, values[0], values[1])
-
-
 def rows_of(i, frames):
     if isinstance(i, int):
         return pl.ds(i * frames, frames)
     return pl.ds(pl.multiple_of(i * frames, frames), frames)
-
-
-def over_both(counts, body):
-    n0, n1 = counts
-    low, high = jnp.minimum(n0, n1), jnp.maximum(n0, n1)
-    longer = (n1 > n0).astype(jnp.int32)
-
-    def both(c, _):
-        body((0, 1), c)
-        return 0
-
-    def one(c, _):
-        body((longer,), c)
-        return 0
-
-    lax.fori_loop(0, low, both, 0)
-    lax.fori_loop(low, high, one, 0)
 
 
 def mask_rows(x, items, frames, tab):
@@ -308,126 +287,13 @@
     def start(self, y, b):
         self.copy(y, b).start()
 
+    def wait_block(self, b):
+        for y in range(self.stage.shape[0]):
+            self.copy(y, b).wait()
+
     def wait(self):
-        for y in range(self.stage.shape[0]):
-            for b in range(self.stage.shape[1]):
-                self.copy(y, b).wait()
-
-
-def ffn_bwd_kernel(layer, items, frames, last, first, subnet, vec, cot_any, dxn_any, r2_any, r1_any, gp_any, g_any, n1b_any,
-                   *rest):
-    (da_o, dr1_o, sums, grads, w_up, w_down, cot, dxn, r2, r1, gp, g, n1b, du, df, acc, da, stage, wsem, sem,
-     gsem, qsem) = rest[(2 if last else 3):]
-    width, units = w_up.shape
-    tab = Table(subnet, items, width)
-    nblk, nch = units // width, units // UNIT_CHUNK
-    loads = [fetch(r2_any, r2, sem.at[0]), fetch(cot_any, cot, sem.at[1])]
-    if not last:
-        loads.append(fetch(dxn_any, dxn, sem.at[2]))
-    p = Ffn(layer, rest[:2], w_up, w_down, wsem)
-    p.start()
-
-    def load_gp(c):
-        cols = pl.ds(pl.multiple_of(c * UNIT_CHUNK, UNIT_CHUNK), UNIT_CHUNK)
-        return pltpu.make_async_copy(gp_any.at[:, cols], gp.at[:, cols], gsem.at[c])
-
-    for c in range(nch):
-        load_gp(c).start()
-    later = [fetch(r1_any, r1, sem.at[3]), fetch(n1b_any, n1b, sem.at[4]), fetch(g_any, g, sem.at[5])]
-    sums[...] = jnp.zeros_like(sums)
-    for o in loads:
-        o.wait()
-    for i in range(items):
-        rr = rows_of(i, frames)
-        cm = lane_mask(width, tab.w[i])
-        if last:
-            dy = jnp.where(tab.skip[i] == 1, 0.0, cot[rr, :].astype(F32))
-        else:
-            dy = jnp.where(tab.skip[i] == 1, cot[rr, :], dxn[rr, :]).astype(F32)
-        xhat, rstd = normed(r2[rr, :], cm, tab.inv[i])
-        dr2, dg, ds = norm_back(dy, xhat, rstd, vec[ROW_G2:ROW_G2 + 1, :], cm, tab.inv[i])
-        dfb = dr2.astype(BF)
-        df[rr, :] = dfb
-        acc[rr, :] = dr2
-        sums[ROW_G2:ROW_G2 + 1, 0:width] += dg
-        sums[ROW_B2:ROW_B2 + 1, 0:width] += ds
-        sums[ROW_DB:ROW_DB + 1, 0:width] += jnp.sum(dfb.astype(F32), axis=0, keepdims=True)
-
-    def chunk(its, c):
-        p.before(c)
-        load_gp(c).wait()
-        cols = pl.ds(pl.multiple_of(c * UNIT_CHUNK, UNIT_CHUNK), UNIT_CHUNK)
-        dgs = [dot_nt(df[rows_of(i, frames), :], w_down[cols, :]) for i in its]
-        dubs = []
-        for i, dg in zip(its, dgs):
-            dub = (dg * gp[rows_of(i, frames), cols].astype(F32)).astype(BF)
-            du[rows_of(i, frames), cols] = dub
-            sums[ROW_UB:ROW_UB + 1, cols] += jnp.sum(dub.astype(F32), axis=0, keepdims=True)
-            dubs.append(dub)
-        for i, dub in zip(its, dubs):
-            acc[rows_of(i, frames), :] += dot_nt(dub, w_up[:, cols])
-
-    over_both(tab.chunks, chunk)
-    p.drain(tab.chunks)
-
-    def drain(c, _):
-        load_gp(c).wait()
-        return 0
-
-    lax.fori_loop(jnp.maximum(tab.chunks[0], tab.chunks[1]), nch, drain, 0)
-    for i in range(items):
-        def blank(c, _, i=i):
-            cols = pl.ds(pl.multiple_of(c * UNIT_CHUNK, UNIT_CHUNK), UNIT_CHUNK)
-            du[rows_of(i, frames), cols] = jnp.zeros((frames, UNIT_CHUNK), BF)
-            return 0
-
-        lax.fori_loop(tab.chunks[i], nch, blank, 0)
-    for o in later:
-        o.wait()
-    quarters = Quarters(stage, grads, qsem, first)
-    rows = stage.shape[3]
-
-    def down_step(f, _):
-        y, par = f // 2, f % 2
-        for s in range(nblk // 2):
-            lanes = pl.ds(pl.multiple_of(f * width + s * 2 * rows, LANES), 2 * rows)
-            res = dot_tn(g[:, lanes], df[...]).astype(BF)
-            for t in (0, 1):
-                stage[y, 2 * s + t, par] = res[t * rows:(t + 1) * rows]
-
-        @pl.when(par == 1)
-        def _():
-            for b in range(nblk):
-                quarters.start(y, b)
-        return 0
-
-    lax.fori_loop(0, 4, down_step, 0)
-    for i in range(items):
-        rr = rows_of(i, frames)
-        cm = lane_mask(width, tab.w[i])
-        xhat, rstd = normed(r1[rr, :], cm, tab.inv[i])
-        d1, dg, ds = norm_back(acc[rr, :], xhat, rstd, vec[ROW_G1:ROW_G1 + 1, :], cm, tab.inv[i])
-        acc[rr, :] = d1
-        dab = d1.astype(BF)
-        da[rr, :] = dab
-        sums[ROW_G1:ROW_G1 + 1, 0:width] += dg
-        sums[ROW_B1:ROW_B1 + 1, 0:width] += ds
-        sums[ROW_OB:ROW_OB + 1, 0:width] += jnp.sum(dab.astype(F32), axis=0, keepdims=True)
-    outs = [fetch(acc, dr1_o, sem.at[6]), fetch(da, da_o, sem.at[7])]
-
-    def up_step(j, _):
-        cols = pl.ds(pl.multiple_of(j * width, LANES), width)
-        for y in (0, 1):
-            res = dot_tn(n1b[:, y * 2 * rows:(y + 1) * 2 * rows], du[:, cols]).astype(BF)
-            for t in (0, 1):
-                stage[y, nblk + j, t] = res[t * rows:(t + 1) * rows]
-            quarters.start(y, nblk + j)
-        return 0
-
-    lax.fori_loop(0, nblk, up_step, 0)
-    quarters.wait()
-    for o in outs:
-        o.wait()
+        for b in range(self.stage.shape[1]):
+            self.wait_block(b)
 
 
 ANY = pl.BlockSpec(memory_space=pl.ANY)
@@ -444,36 +310,6 @@
     return jax.ShapeDtypeStruct(shape, dtype)
 
 
-def run(kernel, name, subnet, vmem, hbm, outs, vmem_outs, scratch, sems, flops, nbytes, alias=None):
-    return pl.pallas_call(
-        kernel,
-        out_shape=tuple(outs),
-        in_specs=[SM] + [VM] * len(vmem) + [ANY] * len(hbm),
-        out_specs=tuple(VM if k in vmem_outs else ANY for k in range(len(outs))),
-        scratch_shapes=[pltpu.VMEM(s, d) for s, d in scratch] + [pltpu.SemaphoreType.DMA(s) for s in sems],
-        input_output_aliases={} if alias is None else {len(vmem) + len(hbm): alias},
-        compiler_params=pltpu.CompilerParams(**PARAMS),
-        cost_estimate=cost(flops, nbytes),
-        name=name,
-    )(subnet, *vmem, *hbm)
-
-
-def ffn_bwd(layer, last, first, blocks, subnet, cot, dxn, r2, r1, gp, g, n1b, vec, weights, grads, items):
-    n, d = cot.shape
-    ff = gp.shape[1]
-    q, nb = d // 4, ff // d
-    more = () if grads is None else (grads,)
-    return run(
-        functools.partial(ffn_bwd_kernel, layer, items, n // items, last, first), "ffn_bwd", subnet, (vec,),
-        (cot, dxn, r2, r1, gp, g, n1b, *weights, *more),
-        [sds((n, d), BF), sds((n, d), F32), sds((8, ff), F32), sds((2, blocks, 2, q, d), BF)], (2,),
-        [((d, ff), BF), ((ff, d), BF), ((n, d), BF), ((n, d), BF), ((n, d), F32), ((n, d), F32), ((n, ff), BF),
-         ((n, ff), BF), ((n, d), BF), ((n, ff), BF), ((n, d), BF), ((n, d), F32), ((n, d), BF),
-         ((2, 2 * nb, 2, q, d), BF)],
-        [(nb, 2), (8,), (ff // UNIT_CHUNK,), (2, 2 * nb)],
-        10 * n * d * ff, 8 * d * ff + n * d * 40, None if grads is None else 3)
-
-
 MESH = pl.DeviceIdType.MESH
 
 
@@ -485,7 +321,7 @@
     barrier = pltpu.get_barrier_semaphore()
     for who in partners:
         pl.semaphore_signal(barrier, inc=1, device_id=who, device_id_type=MESH)
-    pl.semaphore_wait(barrier, len(partners))
+    return lambda: pl.semaphore_wait(barrier, len(partners))
 
 
 class Gather:
@@ -498,8 +334,17 @@
         self.far = jnp.bitwise_xor(self.f, 2)
         self.who = {"c": flip("fsdp", 0), "y": flip("fsdp", 1), "x": flip("pipe", 0), "z": flip("pipe", 1)}
         self.rows, self.width = shards[1].shape[1:]
-        self.chunks = [(l, kind) for l in range(layers) for kind in range(3)]
+        piece, half = self.rows // 4, self.rows // 2
+        self.chunks = []
+        for l in range(layers):
+            if l == 0:
+                self.chunks += [(l, 0, 0, piece // 2), (l, 0, piece // 2, piece // 2)]
+            else:
+                self.chunks += [(l, 0, 0, piece)]
+            self.chunks += [(l, 1, 0, half), (l, 1, half, half)]
+        self.of = lambda l, kind: [n for n, c in enumerate(self.chunks) if c[0] == l and (c[1] > 0) == (kind > 0)]
         self.direct = {n: (None, 1, 0)[n % 3] for n in range(len(self.chunks))}
+        self.direct[1] = None
         self.ids, self.began, self.arrived = {}, [], set()
 
     def at(self, ref, k, layer, row, nrows, col, ncols, quarter):
@@ -511,16 +356,15 @@
         return self.full[w].at[l, pl.ds(pl.multiple_of(self.f * n, 8), n)]
 
     def regions(self, n, ab, k):
-        kind = self.chunks[n][1]
-        d, piece, half = self.width, self.rows // 4, self.rows // 2
+        _, kind, start, count = self.chunks[n]
+        d, piece = self.width, self.rows // 4
         if kind == 0:
             if ab == 0:
-                return [(0, piece * k, piece, 0, 2 * d)]
-            return [(0, piece * k, piece, 2 * d, d), (1, piece * k, piece, 0, d)]
-        row = (kind - 1) * half
+                return [(0, piece * k + start, count, 0, 2 * d)]
+            return [(0, piece * k + start, count, 2 * d, d), (1, piece * k + start, count, 0, d)]
         if ab == 0:
-            return [(2, row, half, pl.multiple_of(k * d, LANES), d)]
-        return [(3, k * self.rows + row, half, 0, d)]
+            return [(2, start, count, pl.multiple_of(k * d, LANES), d)]
+        return [(3, k * self.rows + start, count, 0, d)]
 
     def copies(self, key):
         kind = key[0]
@@ -563,25 +407,21 @@
                 c.wait_recv()
             self.arrived.add(key)
 
-    def tick(self, t):
-        count = len(self.chunks)
-        if t < count:
+    def step(self, k, n):
+        if k == 0:
             for ab in (0, 1):
-                self.start("y", t, ab, 0)
-            if self.direct[t] is not None:
-                self.start("y", t, self.direct[t], 3)
-        n = t - 3
-        if 0 <= n < count:
-            self.landed("x", n, 1, 0)
-            self.landed("z", n, 0, 0)
-            self.start("c", n, 1, 2)
-            self.start("c", n, 0, 1)
-            for ab, link in ((0, "z"), (1, "x")):
-                if self.direct[n] != ab:
-                    self.landed(link, n, ab, 2 if ab == 0 else 1)
-                    self.start("c", n, ab, 3)
-        n = t - 2
-        if 0 <= n < count:
+                self.start("y", n, ab, 0)
+            if self.direct[n] is not None:
+                self.start("y", n, self.direct[n], 3)
+        elif k == 1:
+            for ab in (0, 1):
+                self.landed("y", n, ab, 0)
+            for ab in (0, 1):
+                self.start("x", n, ab, 0)
+                self.start("z", n, ab, 0)
+            for ab in (0, 1):
+                self.start("c", n, ab, 0)
+        elif k == 2:
             self.landed("x", n, 0, 0)
             self.landed("z", n, 1, 0)
             if self.direct[n] != 0:
@@ -593,15 +433,15 @@
                 self.start("c", n, self.direct[n], 3)
             self.start("c", n, 0, 2)
             self.start("c", n, 1, 1)
-        n = t - 1
-        if 0 <= n < count:
-            for ab in (0, 1):
-                self.landed("y", n, ab, 0)
-            for ab in (0, 1):
-                self.start("x", n, ab, 0)
-                self.start("z", n, ab, 0)
-            for ab in (0, 1):
-                self.start("c", n, ab, 0)
+        else:
+            self.landed("x", n, 1, 0)
+            self.landed("z", n, 0, 0)
+            self.start("c", n, 1, 2)
+            self.start("c", n, 0, 1)
+            for ab, link in ((0, "z"), (1, "x")):
+                if self.direct[n] != ab:
+                    self.landed(link, n, ab, 2 if ab == 0 else 1)
+                    self.start("c", n, ab, 3)
 
     def ready(self, n):
         for ab in (0, 1):
@@ -629,6 +469,7 @@
     order = [(k, l) for l in range(layers) for k in range(4)]
     loads = [pltpu.make_async_copy(shards[k].at[l], own[k].at[l], local_sem.at[0, k, l]) for k, l in order]
     stores = [pltpu.make_async_copy(own[k].at[l], gat.place(k, l), local_sem.at[1, k, l]) for k, l in order]
+    met = greet(list(gat.who.values()))
     load_x = fetch(x_any, x, xsem.at[0])
     for c in loads:
         c.start()
@@ -636,10 +477,17 @@
     for k, ref in enumerate(smalls):
         for l in range(layers):
             every[gat.f, l, k:k + 1, 0:ref.shape[1]] = ref[l:l + 1, :].astype(F32)
-    greet(list(gat.who.values()))
+    met()
     gat.start("small", "y", 0)
     gat.start("small", "c", 0)
-    gat.tick(0)
+    step = gat.step
+    before = [(0, 1), (1, 0), (0, 2), (2, 0), (1, 1), (0, 3), (3, 0), (2, 1), (1, 2), (0, 4), (3, 1), (2, 2), (1, 3)]
+    inside = [
+        [{3: [(0, 5), (3, 2), (2, 3), (1, 4)]}, {3: [(3, 4), (2, 5), (1, 6)]}],
+        [{3: [(3, 5), (2, 6)]}, {}],
+    ]
+    after = [[[(0, 6), (3, 3), (2, 4), (1, 5)], []], [[(3, 6)], []]]
+    step(0, 0)
     for c, d in zip(loads, stores):
         c.wait()
         d.start()
@@ -649,8 +497,8 @@
         gat.start("own", 0, k)
     load_x.wait()
     mask_rows(x, items, frames, tab)
-    for t in (1, 2, 3):
-        gat.tick(t)
+    for one in before:
+        step(*one)
     gat.landed("small", "c", 0)
     gat.landed("small", "c", 1)
     rows = gat.rows
@@ -664,49 +512,35 @@
         for k in range(4):
             gat.start("own", l, k)
 
-    last_tick = len(gat.chunks) + 2
-    state = [4]
-
-    def tick_to(t):
-        while state[0] <= min(t, last_tick):
-            gat.tick(state[0])
-            state[0] += 1
-
-    def hook_for(t):
-        def hook():
-            gat.tick(t)
-        return hook
-
-    def reserve():
-        if state[0] > last_tick:
-            return {}
-        t = state[0]
-        state[0] += 1
-        return {3: hook_for(t)}
+    def hooks(l, k):
+        def at(steps):
+            return lambda: [step(*one) for one in steps] and None
+        return {c: at(steps) for c, steps in inside[l][k].items()}
+
+    def need(l, kind):
+        for k in ((2, 3) if kind else (0, 1)):
+            gat.landed("own", l, k)
+        for n in gat.of(l, kind):
+            gat.ready(n)
 
     pending = None
     for l in range(layers):
-        tick_to(3 * l + 3)
-        for k in (0, 1):
-            gat.landed("own", l, k)
-        gat.ready(3 * l)
+        need(l, 0)
         if pending is not None:
             pending[0]()
-        hooks = reserve()
         end_a = attn_front(
-            l, items, frames, tab, vec, (w, x, qkv, pt, ob, r1), full[:2], asem, kept[l][:4], hooks)
-        tick_to(3 * l + 5)
-        for k in (2, 3):
-            gat.landed("own", l, k)
-        gat.ready(3 * l + 1)
-        gat.ready(3 * l + 2)
+            l, items, frames, tab, vec, (w, x, qkv, pt, ob, r1), full[:2], asem, kept[l][:4], hooks(l, 0))
+        for one in after[l][0]:
+            step(*one)
+        need(l, 1)
         if pending is not None:
             pending[1]()
         last = l == layers - 1
-        hooks = reserve()
         end_f = ffn_front(
             l, last, items, frames, tab, vec, ub, (w_up, w_down, r1, x, n1b, g, gp, acc), full[2:], fsem,
-            (*kept[l][4:], out_o if last else x1_o), hooks)
+            (*kept[l][4:], out_o if last else x1_o), hooks(l, 1))
+        for one in after[l][1]:
+            step(*one)
         pending = (end_a, end_f)
     pending[0]()
     pending[1]()
@@ -741,8 +575,18 @@
     return res[:4], res[4], res[5], res[6], res[7], [res[8 + 8 * l:16 + 8 * l] for l in range(layers)]
 
 
+def when(cond):
+    if isinstance(cond, bool):
+        return lambda f: f() if cond else None
+    return pl.when(cond)
+
+
+def both(a, b):
+    return a and b if isinstance(a, bool) else jnp.logical_and(a, b)
+
+
 class Reduce:
-    LOC, RECV = 6, 4
+    LOC, RECV = 6, 6
 
     def __init__(self, count, bits, g, out, refs):
         self.count, self.bits, self.g, self.out = count, bits, g, out
@@ -815,15 +659,15 @@
         self.load(0).start()
 
     def tick(self, t):
-        @pl.when(t + 1 < self.count)
+        @when(t + 1 < self.count)
         def _():
             self.move(0, t + 1).start()
             self.load(t + 1).start()
 
         for k in range(self.total):
-            p = t - k
-
-            @pl.when(jnp.logical_and(p >= 0, p < self.count))
+            p = t - k - min(k, 1)
+
+            @when(both(p >= 0, p < self.count))
             def _(k=k, p=p):
                 self.arrive(k, p)
                 if k + 1 < self.total:
@@ -831,18 +675,18 @@
                 else:
                     self.store(p).start()
 
-        p = t - self.total
-
-        @pl.when(jnp.logical_and(p >= 0, p < self.count))
+        p = t - self.total - 1
+
+        @when(both(p >= 0, p < self.count))
         def _():
             self.store(p).wait()
 
     def ticks(self):
-        return self.count + self.total
+        return self.count + self.total + 1
 
 
 def add_low(a, b):
-    return (a.astype(F32) + b.astype(F32)).astype(BF)
+    return a + b
 
 
 class SumAll:
@@ -865,7 +709,7 @@
                     self.move(j).start()
 
 
-def attn_back(layer, items, frames, tab, src, buf, weights, sems, first, grads, tick, t0, dx_out):
+def attn_back(layer, items, frames, tab, src, buf, weights, sems, first, grads, tick, dx_out):
     qkv_any, pt_any, x_any, ob_any = src
     w, da, dr1, qkv, pt, x, ob, do, dqkv, dx, stage = buf
     wsem, sem, ptsem, qsem = sems
@@ -896,9 +740,10 @@
     qsums = []
 
     def pair(c, _):
-        @pl.when(c % 3 == 0)
-        def _():
-            tick(t0 + c // 3)
+        for at in (0, 3):
+            @pl.when(c == at)
+            def _():
+                tick()
 
         lanes = pl.ds(pl.multiple_of(c * LANES, LANES), LANES)
         ids = lax.broadcasted_iota(jnp.int32, (1, LANES), 1) + c * LANES
@@ -932,8 +777,7 @@
         return 0
 
     lax.fori_loop(0, npair, pair, 0)
-    t0 = t0 + (npair + 2) // 3
-    tick(t0)
+    tick()
     q_sum = jnp.sum(dqkv[:, 0:width].astype(F32), axis=0, keepdims=True)
     for o in later:
         o.wait()
@@ -954,8 +798,9 @@
         return 0
 
     lax.fori_loop(0, 3, in_step, 0)
-    tick(t0 + 1)
     step(ob, da[...], 3)
+    quarters.wait()
+    tick()
     for j in range(3):
         p.wait(j)
 
@@ -971,20 +816,22 @@
         dx[rr, :] = (dr1[rr, :] * lane_mask(width, tab.w[i])).astype(BF)
     if dx_out is not None:
         fetch(dx, dx_out, sem.at[2])
-    quarters.wait()
-    tick(t0 + 2)
-    return t0 + 3, q_sum
-
-
-def ffn_back(layer, items, frames, tab, vec, src, buf, weights, sems, first, grads, tick, t0, sums):
+    return q_sum
+
+
+def ffn_back(layer, last, items, frames, tab, vec, src, buf, weights, sems, first, grads, hooks, sums):
     cot_any, r2_any, r1_any, gp_any, g_any, n1b_any = src
     w_up, w_down, cot, dxn, r, du, g, n1b, df, acc, da, stage = buf
     wsem, sem, gsem, qsem = sems
     width, units = w_up.shape
     nblk, nch = units // width, units // UNIT_CHUNK
+    rows = stage.shape[3]
+    down = Quarters(stage, grads, qsem.at[0], first)
+    up = Quarters(stage, grads, qsem.at[1], first + nblk)
+    loads = [fetch(r2_any, r, sem.at[0]), fetch(cot_any, cot, sem.at[1])]
+    load_g = fetch(g_any, g, sem.at[4])
     p = Ffn(layer, weights, w_up, w_down, wsem)
     p.start()
-    loads = [fetch(r2_any, r, sem.at[0]), fetch(cot_any, cot, sem.at[1])]
 
     def load_gp(c):
         cols = pl.ds(pl.multiple_of(c * UNIT_CHUNK, UNIT_CHUNK), UNIT_CHUNK)
@@ -992,13 +839,16 @@
 
     for c in range(nch):
         load_gp(c).start()
-    later = [fetch(n1b_any, n1b, sem.at[3]), fetch(g_any, g, sem.at[4])]
+    load_n1b = fetch(n1b_any, n1b, sem.at[3])
     for o in loads:
         o.wait()
     for i in range(items):
         rr = rows_of(i, frames)
         cm = lane_mask(width, tab.w[i])
-        dy = jnp.where(tab.skip[i] == 1, cot[rr, :], dxn[rr, :]).astype(F32)
+        if last:
+            dy = jnp.where(tab.skip[i] == 1, 0.0, cot[rr, :].astype(F32))
+        else:
+            dy = jnp.where(tab.skip[i] == 1, cot[rr, :], dxn[rr, :]).astype(F32)
         xhat, rstd = normed(r[rr, :], cm, tab.inv[i])
         dr2, dg, ds = norm_back(dy, xhat, rstd, vec[layer, ROW_G2:ROW_G2 + 1, :], cm, tab.inv[i])
         dfb = dr2.astype(BF)
@@ -1008,9 +858,37 @@
         sums[ROW_B2:ROW_B2 + 1, 0:width] += ds
         sums[ROW_DB:ROW_DB + 1, 0:width] += jnp.sum(dfb.astype(F32), axis=0, keepdims=True)
     load_r1 = fetch(r1_any, r, sem.at[2])
-    tick(t0)
-
-    def chunk(c):
+    hooks["norm"]()
+    load_g.wait()
+
+    for s in range(nblk // 2):
+        def down_step(f, _, s=s):
+            y, par = f // 2, f % 2
+            lanes = pl.ds(pl.multiple_of(f * width + s * 2 * rows, LANES), 2 * rows)
+            res = dot_tn(g[:, lanes], df[...]).astype(BF)
+            for t in (0, 1):
+                stage[y, 2 * s + t, par] = res[t * rows:(t + 1) * rows]
+            return 0
+
+        lax.fori_loop(0, 4, down_step, 0)
+        for b in (2 * s, 2 * s + 1):
+            for y in (0, 1):
+                down.start(y, b)
+        if s == 0:
+            down.wait_block(0)
+            hooks["first"]()
+    down.wait_block(1)
+    hooks["down"]()
+
+    def chunk(c, _):
+        for at in (1, 4):
+            @pl.when(c == at)
+            def _(at=at):
+                if at == 1:
+                    for b in range(2, nblk):
+                        down.wait_block(b)
+                hooks["mid"]()
+
         p.before(c)
         load_gp(c).wait()
         cols = pl.ds(pl.multiple_of(c * UNIT_CHUNK, UNIT_CHUNK), UNIT_CHUNK)
@@ -1023,38 +901,10 @@
             dubs.append(dub)
         for i, dub in enumerate(dubs):
             acc[rows_of(i, frames), :] += dot_nt(dub, w_up[:, cols])
-
-    def one(c, _):
-        @pl.when(jnp.logical_and(c % 3 == 0, c > 0))
-        def _():
-            tick(t0 + c // 3)
-
-        chunk(c)
         return 0
 
-    lax.fori_loop(0, nch, one, 0)
-    t0 = t0 + (nch + 2) // 3
-    tick(t0)
-    for o in later:
-        o.wait()
-    rows = stage.shape[3]
-    down = Quarters(stage, grads, qsem.at[0], first)
-    up = Quarters(stage, grads, qsem.at[1], first + nblk)
-
-    def down_step(f, _):
-        y, par = f // 2, f % 2
-        for s in range(nblk // 2):
-            lanes = pl.ds(pl.multiple_of(f * width + s * 2 * rows, LANES), 2 * rows)
-            res = dot_tn(g[:, lanes], df[...]).astype(BF)
-            for t in (0, 1):
-                stage[y, 2 * s + t, par] = res[t * rows:(t + 1) * rows]
-        return 0
-
-    lax.fori_loop(0, 4, down_step, 0)
-    for y in (0, 1):
-        for b in range(nblk):
-            down.start(y, b)
-    tick(t0 + 1)
+    lax.fori_loop(0, nch, chunk, 0)
+    hooks["chunks"]()
     load_r1.wait()
     for i in range(items):
         rr = rows_of(i, frames)
@@ -1067,8 +917,8 @@
         sums[ROW_G1:ROW_G1 + 1, 0:width] += dg
         sums[ROW_B1:ROW_B1 + 1, 0:width] += ds
         sums[ROW_OB:ROW_OB + 1, 0:width] += jnp.sum(dab.astype(F32), axis=0, keepdims=True)
-    down.wait()
-    tick(t0 + 2)
+    hooks["norm1"]()
+    load_n1b.wait()
 
     def up_step(j, _):
         cols = pl.ds(pl.multiple_of(j * width, LANES), width)
@@ -1081,36 +931,46 @@
 
     lax.fori_loop(0, nblk, up_step, 0)
     up.wait()
-    tick(t0 + 3)
-    return t0 + 4
-
-
-def back_kernel(items, frames, bits, blocks, subnet, vec, s_top, da_any, dr1_any, cot_any, *rest):
-    top, bottom, mid, weights = rest[:4], rest[4:8], rest[8:13], rest[13:17]
-    (dx_o, grads, out, total, w_up, w, da, dr1, pt, x, ob, do, dx, r, du, g, stage, srecv) = rest[18:36]
-    asem, bsem, fsem = rest[36:40], rest[40:44], rest[44:48]
-    red = Reduce(2 * blocks, bits, grads, out, rest[48:58])
-    s_send, s_recv, isem = rest[58:]
+    hooks["up"]()
+
+
+def back_kernel(items, frames, bits, blocks, subnet, vec, cot_any, x0_any, x1_any, *rest):
+    kept, weights = (rest[:8], rest[8:16]), rest[16:20]
+    (dx_o, grads, out, total, w_up, w, da, dr1, pt, x, ob, do, dx, r, du, g, stage, srecv) = rest[20:38]
+    asem, bsem, fsem, gsem = rest[38:42], rest[42:46], rest[46:50], rest[50:54]
+    red = Reduce(2 * blocks, bits, grads, out, rest[54:64])
+    s_send, s_recv = rest[64:]
     width = da.shape[1]
     tab = Table(subnet, items, width)
-    loads = [fetch(da_any, da, isem.at[0]), fetch(dr1_any, dr1, isem.at[1])]
-    greet(red.who)
-    red.begin()
-    total[1] = s_top[...]
-    total[0] = jnp.zeros(total.shape[1:], F32)
+    met = greet(red.who)
+    total[...] = jnp.zeros_like(total)
     nb = w_up.shape[1] // width
     w_att, w_ffn = weights[:2], weights[2:]
-    for o in loads:
-        o.wait()
+    count = [0]
+
+    def tick():
+        red.tick(count[0])
+        count[0] += 1
+
+    def begin():
+        met()
+        red.begin()
+
+    nothing = lambda: None
+    att = lambda l: (kept[l][0], kept[l][1], (x0_any, x1_any)[l], kept[l][2])
+    ffn = lambda l: (cot_any, kept[l][7], kept[l][3], kept[l][6], kept[l][5], kept[l][4])
     buf = (w, da, dr1, du, pt, x, ob, do, g, dx, stage)
-    t, q_sum = attn_back(1, items, frames, tab, top, buf, w_att, asem, 2 * nb, grads, red.tick, 0, None)
-    total[1, ROW_QB:ROW_QB + 1, 0:width] = q_sum
-    w_down = w.reshape(nb * width, width)
-    buf_f = (w_up, w_down, x, dx, r, du, g, ob, do, dr1, da, stage)
-    t = ffn_back(0, items, frames, tab, vec, (cot_any,) + tuple(mid), buf_f, w_ffn, fsem, blocks, grads, red.tick, t, total.at[0])
-    t, q_sum = attn_back(0, items, frames, tab, bottom, buf, w_att, bsem, blocks + 2 * nb, grads, red.tick, t, dx_o)
-    total[0, ROW_QB:ROW_QB + 1, 0:width] = q_sum
+    buf_f = (w_up, w.reshape(nb * width, width), x, dx, r, du, g, ob, do, dr1, da, stage)
+    ffn_back(1, True, items, frames, tab, vec, ffn(1), buf_f, w_ffn, fsem, 0, grads,
+             dict(norm=nothing, first=begin, down=tick, mid=tick, chunks=nothing, norm1=nothing, up=tick), total.at[1])
+    total[1, ROW_QB:ROW_QB + 1, 0:width] = attn_back(
+        1, items, frames, tab, att(1), buf, w_att, asem, 2 * nb, grads, tick, None)
+    ffn_back(0, False, items, frames, tab, vec, ffn(0), buf_f, w_ffn, gsem, blocks, grads,
+             dict(norm=tick, first=nothing, down=nothing, mid=tick, chunks=tick, norm1=tick, up=tick), total.at[0])
+    total[0, ROW_QB:ROW_QB + 1, 0:width] = attn_back(
+        0, items, frames, tab, att(0), buf, w_att, bsem, blocks + 2 * nb, grads, tick, dx_o)
     small = SumAll(red.who, total, srecv, s_send, s_recv)
+    t = count[0]
 
     def rest_of(n, _):
         red.tick(n)
@@ -1121,40 +981,39 @@
     pltpu.make_async_copy(dx, dx_o, bsem[1].at[2]).wait()
 
 
-def back(subnet, vec, s_top, da, dr1, cot, top, bottom, mid, weights, grads, items):
+def back(subnet, vec, cot, x0, x1, kept, weights):
     bits = 0
     while (1 << bits) < lax.axis_size("pipe"):
         bits += 1
     n, d = cot.shape
-    ff = mid[2].shape[1]
-    t = n // items
+    items, _, t, _ = kept[0][1].shape
+    ff = kept[0][5].shape[1]
     rows, nb = d // 4, ff // d
     blocks = 2 * nb + 4
-    small = (2,) + s_top.shape
+    small = (2, 8, ff)
     vm, dma = pltpu.VMEM, pltpu.SemaphoreType.DMA
     square = vm((n, d), BF)
-    hbm = (da, dr1, cot, *top, *bottom, *mid, *weights, grads)
+    hbm = (cot, x0, x1, *kept[0], *kept[1], *weights)
     asems = [dma((4,)), dma((6,)), dma((d // LANES,)), dma((2, 4))]
+    fsems = [dma((nb, 2)), dma((5,)), dma((ff // UNIT_CHUNK,)), dma((2, 2, nb))]
     return pl.pallas_call(
         functools.partial(back_kernel, items, t, bits, blocks),
-        out_shape=(sds((n, d), BF), sds(grads.shape, BF), sds((2 * blocks, rows, d), BF), sds(small, F32)),
-        in_specs=[SM, VM, VM] + [ANY] * len(hbm),
+        out_shape=(sds((n, d), BF), sds((2, 2 * blocks, 2, rows, d), BF), sds((2 * blocks, rows, d), BF), sds(small, F32)),
+        in_specs=[SM, VM] + [ANY] * len(hbm),
         out_specs=(ANY, ANY, ANY, VM),
         scratch_shapes=[
             vm((d, ff), BF), vm((4, d, d), BF), square, vm((n, d), F32), vm((3, items, 2, t, t), BF),
             square, square, square, square, vm((n, d), F32), vm((n, ff), BF), vm((n, ff), BF),
             vm((2, 4, 2, rows, d), BF), vm((2 + bits,) + small, F32),
-            *asems, *asems, dma((nb, 2)), dma((5,)), dma((ff // UNIT_CHUNK,)), dma((2, 2, nb)),
-            *Reduce.scratch(bits, 2 * blocks, rows, d), dma((2 + bits,)), dma((2 + bits,)), dma((2,)),
+            *asems, *asems, *fsems, *fsems, *Reduce.scratch(bits, 2 * blocks, rows, d), dma((2 + bits,)), dma((2 + bits,)),
         ],
-        input_output_aliases={2 + len(hbm): 1},
         compiler_params=pltpu.CompilerParams(collective_id=1, has_side_effects=True, vmem_limit_bytes=60 * 2 ** 20),
         name="back",
-    )(subnet, vec, s_top, *hbm)
-
-
-def finish_kernel(layers, red, total, g_in, g_out, g_up, g_down, *rest):
-    vecs, (bf, f32, sem_in, sem_out) = rest[:8], rest[8:]
+    )(subnet, vec, *hbm)
+
+
+def finish_kernel(layers, red, rows_a, rows_b, total, g_in, g_out, g_up, g_down, *rest):
+    vecs, passed, (bf, f32, keep, sem_in, sem_out, sem_rows) = rest[:8], rest[8:10], rest[10:]
     f = lax.axis_index("fsdp")
     blocks = bf.shape[0]
     rows, d = bf.shape[1:]
@@ -1172,8 +1031,13 @@
 
     loads = [pltpu.make_async_copy(red.at[p], bf.at[p], sem_in.at[p]) for p in range(blocks)]
     stores = [pltpu.make_async_copy(f32.at[p], target(layers - 1 - p // per, p % per), sem_out.at[p]) for p in range(blocks)]
-    for c in loads:
+    rows_in = [pltpu.make_async_copy(a, keep.at[k], sem_rows.at[0, k]) for k, a in enumerate((rows_a, rows_b))]
+    rows_out = [pltpu.make_async_copy(keep.at[k], a, sem_rows.at[1, k]) for k, a in enumerate(passed)]
+    for c in rows_in + loads:
         c.start()
+    for came, goes in zip(rows_in, rows_out):
+        came.wait()
+        goes.start()
     for q in range(4):
         @pl.when(f == q)
         def _(q=q):
@@ -1185,25 +1049,27 @@
         loads[p].wait()
         f32[p] = bf[p].astype(F32)
         stores[p].start()
-    for c in stores:
+    for c in stores + rows_out:
         c.wait()
 
 
-def finish(red, total):
+def finish(red, rows_a, rows_b, total):
     blocks, rows, d = red.shape
     layers = total.shape[0]
     nb = (blocks // layers - 4) // 2
     return pl.pallas_call(
         functools.partial(finish_kernel, layers),
         out_shape=(sds((layers, rows, 3 * d), F32), sds((layers, rows, d), F32), sds((layers, rows, nb * d), F32),
-                   sds((layers, nb * rows, d), F32)) + (sds((layers, rows), F32),) * 7 + (sds((layers, d), F32),),
-        in_specs=[ANY, VM],
-        out_specs=(ANY,) * 4 + (VM,) * 8,
-        scratch_shapes=[pltpu.VMEM(red.shape, BF), pltpu.VMEM(red.shape, F32), pltpu.SemaphoreType.DMA((blocks,)),
-                        pltpu.SemaphoreType.DMA((blocks,))],
+                   sds((layers, nb * rows, d), F32)) + (sds((layers, rows), F32),) * 7 + (sds((layers, d), F32),)
+        + (sds(rows_a.shape, BF), sds(rows_b.shape, BF)),
+        in_specs=[ANY, ANY, ANY, VM],
+        out_specs=(ANY,) * 4 + (VM,) * 8 + (ANY, ANY),
+        scratch_shapes=[pltpu.VMEM(red.shape, BF), pltpu.VMEM(red.shape, F32), pltpu.VMEM((2,) + rows_a.shape, BF),
+                        pltpu.SemaphoreType.DMA((blocks,)), pltpu.SemaphoreType.DMA((blocks,)),
+                        pltpu.SemaphoreType.DMA((2, 2))],
         compiler_params=pltpu.CompilerParams(**PARAMS),
         name="finish",
-    )(red, total)
+    )(red, rows_a, rows_b, total)
 
 
 def local(
@@ -1217,19 +1083,11 @@
     smalls = (q_bias, out_bias, norm1_gain, norm1_bias, down_bias, norm2_gain, norm2_bias, up_bias)
     n = items * frames
     weights, vec, ub, x1, layer_out, kept = fore(subnet, smalls, frames_in, (attn_in, attn_out, ffn_up, ffn_down))
-    layer_out = layer_out.reshape(frames_in.shape)
     cot = out_cotangent.reshape(n, width)
-    qkv1, pt1, ob1, r1, n1b, g, gp, r2 = kept[1]
-    da, dr1, s_top, grads = ffn_bwd(
-        1, True, 0, 2 * (2 * nb + 4), subnet, cot, cot, r2, r1, gp, g, n1b, vec[1], weights[2:], None, items)
-    x0 = frames_in.reshape(n, width)
-    qkv0, pt0, ob0, r1, n1b, g, gp, r2 = kept[0]
-    dx, _, red, total = back(
-        subnet, vec, s_top, da, dr1, cot, (qkv1, pt1, x1, ob1), (qkv0, pt0, x0, ob0), (r2, r1, gp, g, n1b), weights, grads,
-        items)
-    dx = dx.reshape(frames_in.shape)
-    g_in, g_out, g_up, g_down, g_qb, g_ob, g_g1, g_b1, g_db, g_g2, g_b2, g_ub = finish(red, total)
-    return (layer_out, dx, g_in, g_qb, g_out, g_ob, g_g1, g_b1, g_up, g_ub, g_down, g_db, g_g2, g_b2)
+    dx, _, red, total = back(subnet, vec, cot, frames_in.reshape(n, width), x1, kept, weights)
+    g_in, g_out, g_up, g_down, g_qb, g_ob, g_g1, g_b1, g_db, g_g2, g_b2, g_ub, layer_out, dx = finish(
+        red, layer_out, dx, total)
+    return (layer_out.reshape(frames_in.shape), dx.reshape(frames_in.shape), g_in, g_qb, g_out, g_ob, g_g1, g_b1, g_up, g_ub, g_down, g_db, g_g2, g_b2)
 
 
 def solution(mesh):

time: 346 us -> 327 us (0.945)
  Pallas kernels: 338 us -> 323 us
  local copies, waits for them, and re-layouts: 4.04 us -> 0 us
    pallas_call x1 -> x0, Pallas kernels: 28.1 us -> none  [run(): pl.pallas_call(kernel, out_shape=tuple(outs), in_specs=[SM] + [VM] * len(...]
    pallas_call x1, Pallas kernels: 204 us -> 213 us  [back(): pl.pallas_call(functools.partial(back_kernel, items, t, bits, blocks), ou...]
where the time goes in v1:
time: 327 us; the launch traced here: 324 us
  Pallas kernels  323 us (99%)
    pallas_call x1, Pallas kernels, back(): pl.pallas_call(functools.partial(back_kernel, items, t, bits, blocks), ou...  213 us
    pallas_call x1, Pallas kernels, fore(): pl.pallas_call(functools.partial(fore_kernel, layers, items, t), out_shap...  98.9 us
    pallas_call x1, Pallas kernels, finish(): pl.pallas_call(functools.partial(finish_kernel, layers), out_shape=(sds((...  11.1 us

profile of v1, /device:TPU:0, one launch (start us, length us, event | category | flops | bytes accessed | tf_op | source)
XLA Modules:
  0.0 324.5 jit_solution(15947876578339715546)
XLA Ops:
  0.6 98.9 %fore.1 = (bf16[2,768,2304]{2,1,0:T(8,128)(2,1)}, bf16[2,768,768]{2,1,0:T(8,128)(2,1)}, bf16[2,768,3072]{2,1,0:T(8,128)(2,1)}, bf16[2,3072,768]{2,1,0:T(8,128)(2...) custom-call(s32[4,4]{1,0:T(4,128)} %subnet.3, ...), custom_call_target="tpu_custom_call" | custom-call | tf_op jit(solution)/shard_map/fore/pallas_call | solution.py:561
  99.6 213.4 %back.1 = (bf16[768,768]{1,0:T(8,128)(2,1)}, bf16[2,24,2,192,768]{4,3,2,1,0:T(8,128)(2,1)}, bf16[24,192,768]{2,1,0:T(8,128)(2,1)}, f32[2,8,3072]{2,1,0:T(8,128)}) custom-call(s32[4,4]{1,0:T(4,128)} %subnet.3, f32[2,8,768]{2,1,0:T(8,128)} %get-tuple-element.54.vec, bf16[768,768]{1,0:T(8,128)(2,1)} %bitcast.6, bf16[768,768]{1,0:T(8,128)(2,1)} %bitcast.5, ...), custom_call_target="tpu_custom_call" | custom-call | tf_op jit(solution)/shard_map/back/pallas_call | solution.py:999
  313.0 11.1 %finish.1 = (f32[2,192,2304]{2,1,0:T(8,128)}, f32[2,192,768]{2,1,0:T(8,128)}, f32[2,192,3072]{2,1,0:T(8,128)}, f32[2,768,768]{2,1,0:T(8,128)}, f32[2,192]{1,0:T(...) custom-call(bf16[24,192,768]{2,1,0:T(8,128)(2,1)} %get-tuple-element, ...), custom_call_target="tpu_custom_call" | custom-call | tf_op jit(solution)/shard_map/finish/pallas_call | solution.py:1060

commit v2 on v1

--- a/solution.py
+++ b/solution.py
@@ -12,6 +12,7 @@
 EPSILON = 1e-05
 LANES = 128
 UNIT_CHUNK = 512
+FRONT_CHUNK = 768
 BF = jnp.bfloat16
 F32 = jnp.float32
 
@@ -68,11 +69,11 @@
 
 
 class Ffn:
-    def __init__(self, layer, refs, w_up, w_down, sems):
+    def __init__(self, layer, refs, w_up, w_down, sems, chunk):
         up, down = refs
         d = w_up.shape[0]
         self.blocks = w_up.shape[1] // d
-        self.first = [b * d // UNIT_CHUNK for b in range(self.blocks)]
+        self.first = [b * d // chunk for b in range(self.blocks)]
         self.copies = [(
             pltpu.make_async_copy(up.at[layer, :, pl.ds(b * d, d)], w_up.at[:, pl.ds(b * d, d)], sems.at[b, 0]),
             pltpu.make_async_copy(down.at[layer, pl.ds(b * d, d)], w_down.at[pl.ds(b * d, d)], sems.at[b, 1]),
@@ -214,8 +215,8 @@
     wsem, sem, gsem = sems
     n1b_o, g_o, gp_o, r2_o, out_o = outs
     width, units = w_up.shape
-    nch = units // UNIT_CHUNK
-    p = Ffn(layer, weights, w_up, w_down, wsem)
+    nch = units // FRONT_CHUNK
+    p = Ffn(layer, weights, w_up, w_down, wsem, FRONT_CHUNK)
     p.start()
     cms = [lane_mask(width, n) for n in tab.w]
     for i in range(items):
@@ -227,7 +228,7 @@
     done = [fetch(n1b, n1b_o, sem.at[0])]
 
     def store(k, c):
-        cols = pl.ds(pl.multiple_of(c * UNIT_CHUNK, UNIT_CHUNK), UNIT_CHUNK)
+        cols = pl.ds(pl.multiple_of(c * FRONT_CHUNK, FRONT_CHUNK), FRONT_CHUNK)
         ref, out = ((g, g_o), (gp, gp_o))[k]
         return pltpu.make_async_copy(ref.at[:, cols], out.at[:, cols], gsem.at[k, c])
 
@@ -238,8 +239,8 @@
                 hook()
 
         p.before(c)
-        cols = pl.ds(pl.multiple_of(c * UNIT_CHUNK, UNIT_CHUNK), UNIT_CHUNK)
-        ids = lax.broadcasted_iota(jnp.int32, (1, UNIT_CHUNK), 1) + c * UNIT_CHUNK
+        cols = pl.ds(pl.multiple_of(c * FRONT_CHUNK, FRONT_CHUNK), FRONT_CHUNK)
+        ids = lax.broadcasted_iota(jnp.int32, (1, FRONT_CHUNK), 1) + c * FRONT_CHUNK
         us = [dot_nn(n1b[rows_of(i, frames), :], w_up[:, cols]) for i in range(items)]
         gbs = []
         for i, u in enumerate(us):
@@ -483,7 +484,7 @@
     step = gat.step
     before = [(0, 1), (1, 0), (0, 2), (2, 0), (1, 1), (0, 3), (3, 0), (2, 1), (1, 2), (0, 4), (3, 1), (2, 2), (1, 3)]
     inside = [
-        [{3: [(0, 5), (3, 2), (2, 3), (1, 4)]}, {3: [(3, 4), (2, 5), (1, 6)]}],
+        [{3: [(0, 5), (3, 2), (2, 3), (1, 4)]}, {2: [(3, 4), (2, 5), (1, 6)]}],
         [{3: [(3, 5), (2, 6)]}, {}],
     ]
     after = [[[(0, 6), (3, 3), (2, 4), (1, 5)], []], [[(3, 6)], []]]
@@ -567,7 +568,7 @@
             vm((4, layers, 8, d), F32), *[vm(w.shape, BF) for w in weights], dma((200,)), dma((200,)), dma((2, 4, layers)),
             vm((4, d, d), BF), square, vm((3, n, d), BF), vm((items, HEADS, t, t), BF), square, vm((n, d), F32),
             vm((d, ff), BF), vm((ff, d), BF), square, vm((n, ff), BF), vm((n, ff), BF), vm((n, d), F32),
-            dma((4,)), dma((5,)), dma((d // LANES,)), dma((ff // d, 2)), dma((3,)), dma((2, ff // UNIT_CHUNK)), dma((1,)),
+            dma((4,)), dma((5,)), dma((d // LANES,)), dma((ff // d, 2)), dma((3,)), dma((2, ff // FRONT_CHUNK)), dma((1,)),
         ],
         compiler_params=pltpu.CompilerParams(collective_id=0, has_side_effects=True, vmem_limit_bytes=60 * 2 ** 20),
         name="fore",
@@ -830,7 +831,7 @@
     up = Quarters(stage, grads, qsem.at[1], first + nblk)
     loads = [fetch(r2_any, r, sem.at[0]), fetch(cot_any, cot, sem.at[1])]
     load_g = fetch(g_any, g, sem.at[4])
-    p = Ffn(layer, weights, w_up, w_down, wsem)
+    p = Ffn(layer, weights, w_up, w_down, wsem, UNIT_CHUNK)
     p.start()
 
     def load_gp(c):

time: 327 us -> 327 us (level)
  no operation moved by 1% of the time
where the time goes in v2:
time: 327 us; the launch traced here: 324 us
  Pallas kernels  323 us (99%)
    pallas_call x1, Pallas kernels, back(): pl.pallas_call(functools.partial(back_kernel, items, t, bits, blocks), ou...  215 us
    pallas_call x1, Pallas kernels, fore(): pl.pallas_call(functools.partial(fore_kernel, layers, items, t), out_shap...  97.5 us
    pallas_call x1, Pallas kernels, finish(): pl.pallas_call(functools.partial(finish_kernel, layers), out_shape=(sds((...  11.1 us

profile of v2, /device:TPU:0, one launch (start us, length us, event | category | flops | bytes accessed | tf_op | source)
XLA Modules:
  0.0 324.2 jit_solution(9685890248100867850)
XLA Ops:
  0.6 97.5 %fore.1 = (bf16[2,768,2304]{2,1,0:T(8,128)(2,1)}, bf16[2,768,768]{2,1,0:T(8,128)(2,1)}, bf16[2,768,3072]{2,1,0:T(8,128)(2,1)}, bf16[2,3072,768]{2,1,0:T(8,128)(2...) custom-call(s32[4,4]{1,0:T(4,128)} %subnet.3, ...), custom_call_target="tpu_custom_call" | custom-call | tf_op jit(solution)/shard_map/fore/pallas_call | solution.py:562
  98.1 214.5 %back.1 = (bf16[768,768]{1,0:T(8,128)(2,1)}, bf16[2,24,2,192,768]{4,3,2,1,0:T(8,128)(2,1)}, bf16[24,192,768]{2,1,0:T(8,128)(2,1)}, f32[2,8,3072]{2,1,0:T(8,128)}) custom-call(s32[4,4]{1,0:T(4,128)} %subnet.3, f32[2,8,768]{2,1,0:T(8,128)} %get-tuple-element.54.vec, bf16[768,768]{1,0:T(8,128)(2,1)} %bitcast.6, bf16[768,768]{1,0:T(8,128)(2,1)} %bitcast.5, ...), custom_call_target="tpu_custom_call" | custom-call | tf_op jit(solution)/shard_map/back/pallas_call | solution.py:1000
  312.7 11.1 %finish.1 = (f32[2,192,2304]{2,1,0:T(8,128)}, f32[2,192,768]{2,1,0:T(8,128)}, f32[2,192,3072]{2,1,0:T(8,128)}, f32[2,768,768]{2,1,0:T(8,128)}, f32[2,192]{1,0:T(...) custom-call(bf16[24,192,768]{2,1,0:T(8,128)(2,1)} %get-tuple-element, ...), custom_call_target="tpu_custom_call" | custom-call | tf_op jit(solution)/shard_map/finish/pallas_call | solution.py:1061
